TPU v7x, 128 devices: a whole 4x4x4 slice. The times are simulated.
128 devices in a mesh: chan: 16 (over z, y), seg: 4 (over x_hi, core), lag: 2 (over x_lo).
Axes of the slice: x: 4 (x_hi: 2, x_lo: 2; x = x_hi * 2 + x_lo), y: 4, z: 4, core: 2. Of those that a mesh axis runs over, the one named last changes fastest.
Arguments:
- spectra: bfloat16 [4, 10000, 2, 6144], P('seg', 'chan', None, 'lag'), may hold values from -6 to 6
- pair_local: int32 [16, 3, 256], replicated, may hold values from 0 to 624
- pair_partner: int32 [16, 3, 256], replicated, may hold values from 0 to 624, as said below
- pair_bin: int32 [16, 3, 256], replicated, may hold values from 0 to 1
- pair_owner: int32 [16, 3, 256], replicated, may hold values 0 or 1
- pair_count: int32 [16, 3], replicated, may hold values from 64 to 256, as said below
Outputs:
- stacks: float32 [10000, 2, 2048], P('chan', None, 'lag')
Inputs may be any that keep to these rules, and one draw needn't show every extreme that they name: `pair_partner`: in round 0 the two channels of a pair differ. `pair_count`: some block reaches 256 in some round.
All inputs are finite; a program needn't handle non-finite values.
Results may differ from a plain program's by a relative error of at most 0.0065.
Values may be sent and summed in bfloat16 or wider, within the bound.
No kernel may reach another device: no remote copies, remote signals or barrier semaphores. Data moves between devices by JAX's collectives and lax.ppermute only.
A program may use at most 128 MiB of HBM per device.

v0:
```python
import math

import jax
import jax.numpy as jnp
from jax import lax
from jax.sharding import PartitionSpec as P

FREQ = 6144
LAGS = 2048
ROUNDS = 3
BINS = 2


def shifted(block, axis, distance):
    devices = range(lax.axis_size(axis))
    route = [((i - distance) % len(devices), i) for i in devices]
    return lax.ppermute(block, axis, route)


def one_hot_rows(target_rows, mask_rows, total_rows):
    row_ids = jnp.arange(total_rows, dtype=jnp.int32)[:, None]
    return ((row_ids == target_rows[None, :]) & mask_rows[None, :]).astype(jnp.float32)


def bin_rows(selector, corr):
    return lax.dot_general(
        selector,
        corr,
        (((1,), (1,)), ((), ())),
        precision=lax.Precision.HIGHEST,
        preferred_element_type=jnp.float32,
    )


def per_device(spectra, pair_local, pair_partner, pair_bin, pair_owner, pair_count):
    block_index = lax.axis_index("chan")
    lag_index = lax.axis_index("lag")
    own_block = spectra[0]
    block_chans = own_block.shape[0]
    half_freq = own_block.shape[2]
    half_lags = LAGS // lax.axis_size("lag")
    total_rows = block_chans * BINS
    slot_count = pair_local.shape[2]
    freq_index = lag_index * half_freq + jnp.arange(half_freq, dtype=jnp.int32) + 1
    corr_scale = FREQ ** (-0.5)
    slot_ids = jnp.arange(slot_count, dtype=jnp.int32)
    local_stack = jnp.zeros((total_rows, half_lags), jnp.float32)
    for round_index in range(ROUNDS):
        first_index = pair_local[block_index, round_index]
        second_index = pair_partner[block_index, round_index]
        first = jnp.take(own_block, first_index, axis=0).astype(jnp.float32)
        if round_index == 0:
            second = jnp.take(own_block, second_index, axis=0).astype(jnp.float32)
        else:
            partner_block = shifted(own_block, "chan", -round_index)
            second = jnp.take(partner_block, second_index, axis=0).astype(jnp.float32)
        cross_real = first[:, 0] * second[:, 0] + first[:, 1] * second[:, 1]
        cross_imag = first[:, 1] * second[:, 0] - first[:, 0] * second[:, 1]
        cross = jnp.concatenate([cross_real, cross_imag], axis=1).astype(jnp.bfloat16)
        block_rows = math.gcd(lax.axis_size("lag") * half_lags, 512)

        def one_block(offset):
            taus = offset + jnp.arange(block_rows, dtype=jnp.int32) - LAGS // 2
            phase = jnp.mod(taus[:, None] * freq_index[None, :], 2 * FREQ)
            angle = phase.astype(jnp.float32) * (math.pi / FREQ)
            table = jnp.concatenate([jnp.cos(angle), -jnp.sin(angle)], axis=1).astype(jnp.bfloat16)
            return (
                lax.dot_general(
                    table, cross, (((1,), (1,)), ((), ())), preferred_element_type=jnp.float32
                )
                * corr_scale
            )

        offsets = (
            jnp.arange(lax.axis_size("lag") * half_lags // block_rows, dtype=jnp.int32) * block_rows
        )
        corr = lax.psum_scatter(
            lax.map(one_block, offsets).reshape(lax.axis_size("lag") * half_lags, slot_count),
            "lag",
            scatter_dimension=0,
            tiled=True,
        )
        live = slot_ids < pair_count[block_index, round_index]
        owners = pair_owner[block_index, round_index]
        bins_now = pair_bin[block_index, round_index]
        own_rows = jnp.where(owners == 0, first_index, second_index) * BINS + bins_now
        if round_index == 0:
            local_stack = bin_rows(one_hot_rows(own_rows, live, total_rows), corr)
        else:
            mine_rows = first_index * BINS + bins_now
            local_stack = local_stack + bin_rows(
                one_hot_rows(mine_rows, live & (owners == 0), total_rows), corr
            )
            partner_rows = second_index * BINS + bins_now
            partner_stack = bin_rows(
                one_hot_rows(partner_rows, live & (owners == 1), total_rows), corr
            )
            local_stack = local_stack + shifted(partner_stack, "chan", round_index)
    local_stack = lax.psum(local_stack, "seg")
    return local_stack.reshape(block_chans, BINS, half_lags)


def solution(mesh):
    return jax.shard_map(
        per_device,
        mesh=mesh,
        in_specs=(P("seg", "chan", None, "lag"), P(), P(), P(), P(), P()),
        out_specs=P("chan", None, "lag"),
        check_vma=False,
    )
```

profile of v0, /device:TPU:1, one launch (start us, length us, event | category | flops | bytes accessed | tf_op | source)
XLA Modules:
  0.0 1053.5 jit_solution(12858665571062625390)
XLA Ops:
  16.7 16.3 %gather_fusion.2 = bf16[256,2,3072]{2,1,0:T(2,128)(2,1)S(1)} fusion(bf16[625,2,3072]{2,1,0:T(2,128)(2,1)} %bitcast.81, s32[1024]{0:T(1024)S(1)} %pad_clamp_fusion.3), kind=kCustom, calls=%fused_computation.2.clone | custom fusion | bytes 6292480 | tf_op jit(solution)/shard_map/jit(_take)/gather | solution.py:51
  35.0 16.2 %gather_fusion = bf16[256,2,3072]{2,1,0:T(2,128)(2,1)} fusion(bf16[625,2,3072]{2,1,0:T(2,128)(2,1)} %bitcast.82, s32[1024]{0:T(1024)S(1)} %get-tuple-element.328), kind=kCustom, calls=%fused_computation.clone | custom fusion | bytes 6292480 | tf_op jit(solution)/shard_map/jit(_take)/gather | solution.py:51
  51.2 16.5 %gather_fusion.1 = bf16[256,2,3072]{2,1,0:T(2,128)(2,1)} fusion(bf16[625,2,3072]{2,1,0:T(2,128)(2,1)} %bitcast.83, s32[1024]{0:T(1024)S(1)} %get-tuple-element.327), kind=kCustom, calls=%fused_computation.1.clone | custom fusion | bytes 6292480 | tf_op jit(solution)/shard_map/jit(_take)/gather | solution.py:53
  68.2 16.6 %gather_fusion.4 = bf16[256,2,3072]{2,1,0:T(2,128)(2,1)} fusion(bf16[625,2,3072]{2,1,0:T(2,128)(2,1)} %bitcast.84, s32[1024]{0:T(1024)S(1)} %pad_clamp_fusion.1), kind=kCustom, calls=%fused_computation.4.clone | custom fusion | bytes 6292480 | tf_op jit(solution)/shard_map/jit(_take)/gather | solution.py:51
  101.6 240.8 %collective-permute-done = bf16[625,2,3072]{2,1,0:T(2,128)(2,1)} collective-permute-done((bf16[625,2,3072]{2,1,0:T(2,128)(2,1)}, bf16[625,2,3072]{2,1,0:T(2,128)(2,1)}, u32[]{:S(2)}, u32[]{:S(2)}) %collective-permute-start) | collective-permute-done | bytes 7680032 | tf_op jit(solution)/shard_map/ppermute | solution.py:17
  342.4 16.5 %gather_fusion.3 = bf16[256,2,3072]{2,1,0:T(2,128)(2,1)} fusion(bf16[625,2,3072]{2,1,0:T(2,128)(2,1)} %collective-permute-done, s32[1024]{0:T(1024)S(1)} %pad_clamp_fusion.2), kind=kCustom, calls=%fused_computation.3.clone | custom fusion | bytes 6292480 | tf_op jit(solution)/shard_map/jit(_take)/gather | solution.py:56
  358.9 7.6 fusion.66
  366.6 12.3 %add_convert_fusion.1 = (bf16[256,1,3072]{2,1,0:T(2,128)(2,1)S(1)}, bf16[256,1,3072]{2,1,0:T(2,128)(2,1)S(1)}) fusion(f32[256,2,3072]{2,1,0:T(2,128)} %fusion.66, f32[256,2,3072]{2,1,0:T(2,128)S(1)} %bitcast.78), kind=kLoop, calls=%fused_computation.85 | loop fusion | flops 6291456 | bytes 15728640 | tf_op jit(solution)/shard_map/convert.13
  381.9 118.2 %while.40 = (s32[]{:T(128)}, f32[4,512,256]{2,1,0:T(8,128)S(1)}, s32[4]{0:T(128)S(1)}, bf16[256,6144]{1,0:T(8,128)(2,1)}, s32[]{:T(128)}, /*index=5*/s32[]{:T(128)}) while((s32[]{:T(128)}, f32[4,512,256]{2,1,0:T(8,128)S(1)}, s32[4]{0:T(128)S(1)}, bf16[256,6144]{1,0:T(8,128)(2,1)}, s32[]{:T(128)}, /*index=5*/s32[]{:T(128)}) %tuple.118), condition=%wide.region_4.6_spmd.clone, body=%wide.region_3.5_spmd.clone.sunk | while | flops 1642208256 | bytes 28864632 | solution.py:78
  383.3 26.3 %cosine_convert_fusion.7 = (bf16[512,3072]{1,0:T(8,128)(2,1)S(1)}, bf16[512,3072]{1,0:T(8,128)(2,1)S(1)}) fusion(s32[3072]{0:T(1024)S(1)} %add_add_fusion.15, s32[512]{0:T(512)S(1)} %add_add_fusion.16), kind=kLoop, calls=%fused_computation.36.clone.1 | loop fusion | flops 18874368 | bytes 6305792 | tf_op jit(solution)/shard_map/convert.2
  412.8 26.3 %cosine_convert_fusion.7 = (bf16[512,3072]{1,0:T(8,128)(2,1)S(1)}, bf16[512,3072]{1,0:T(8,128)(2,1)S(1)}) fusion(s32[3072]{0:T(1024)S(1)} %add_add_fusion.15, s32[512]{0:T(512)S(1)} %add_add_fusion.16), kind=kLoop, calls=%fused_computation.36.clone.1 | loop fusion | flops 18874368 | bytes 6305792 | tf_op jit(solution)/shard_map/convert.2
  442.4 26.3 %cosine_convert_fusion.7 = (bf16[512,3072]{1,0:T(8,128)(2,1)S(1)}, bf16[512,3072]{1,0:T(8,128)(2,1)S(1)}) fusion(s32[3072]{0:T(1024)S(1)} %add_add_fusion.15, s32[512]{0:T(512)S(1)} %add_add_fusion.16), kind=kLoop, calls=%fused_computation.36.clone.1 | loop fusion | flops 18874368 | bytes 6305792 | tf_op jit(solution)/shard_map/convert.2
  471.9 26.3 %cosine_convert_fusion.7 = (bf16[512,3072]{1,0:T(8,128)(2,1)S(1)}, bf16[512,3072]{1,0:T(8,128)(2,1)S(1)}) fusion(s32[3072]{0:T(1024)S(1)} %add_add_fusion.15, s32[512]{0:T(512)S(1)} %add_add_fusion.16), kind=kLoop, calls=%fused_computation.36.clone.1 | loop fusion | flops 18874368 | bytes 6305792 | tf_op jit(solution)/shard_map/convert.2
  501.7 16.7 %gather_fusion.5 = bf16[256,2,3072]{2,1,0:T(2,128)(2,1)} fusion(bf16[625,2,3072]{2,1,0:T(2,128)(2,1)} %collective-permute-done.2, s32[1024]{0:T(1024)S(1)} %pad_clamp_fusion), kind=kCustom, calls=%fused_computation.5.clone | custom fusion | bytes 6292480 | tf_op jit(solution)/shard_map/jit(_take)/gather | solution.py:56
  518.4 7.6 fusion.68
  526.0 12.4 %add_convert_fusion = (bf16[256,1,3072]{2,1,0:T(2,128)(2,1)S(1)}, bf16[256,1,3072]{2,1,0:T(2,128)(2,1)S(1)}) fusion(f32[256,2,3072]{2,1,0:T(2,128)} %fusion.68, f32[256,2,3072]{2,1,0:T(2,128)S(1)} %bitcast.76), kind=kLoop, calls=%fused_computation.83 | loop fusion | flops 6291456 | bytes 15728640 | tf_op jit(solution)/shard_map/convert.9
  542.8 121.2 %while.41 = (s32[]{:T(128)}, f32[4,512,256]{2,1,0:T(8,128)}, s32[4]{0:T(128)S(1)}, bf16[256,6144]{1,0:T(8,128)(2,1)}, s32[]{:T(128)}, /*index=5*/s32[]{:T(128)}) while((s32[]{:T(128)}, f32[4,512,256]{2,1,0:T(8,128)}, s32[4]{0:T(128)S(1)}, bf16[256,6144]{1,0:T(8,128)(2,1)}, s32[]{:T(128)}, /*index=5*/s32[]{:T(128)}) %tuple.132), condition=%wide.region_7.9_spmd.clone, body=%wide.region_6.8_spmd.clone.sunk | while | flops 1642208256 | bytes 28865140 | solution.py:78
  544.4 26.3 %cosine_convert_fusion.8 = (bf16[512,3072]{1,0:T(8,128)(2,1)S(1)}, bf16[512,3072]{1,0:T(8,128)(2,1)S(1)}) fusion(s32[3072]{0:T(1024)S(1)} %add_add_fusion.17, s32[512]{0:T(512)S(1)} %add_add_fusion.18), kind=kLoop, calls=%fused_computation.55.clone.1 | loop fusion | flops 18874368 | bytes 6305792 | tf_op jit(solution)/shard_map/convert.4
  574.6 26.3 %cosine_convert_fusion.8 = (bf16[512,3072]{1,0:T(8,128)(2,1)S(1)}, bf16[512,3072]{1,0:T(8,128)(2,1)S(1)}) fusion(s32[3072]{0:T(1024)S(1)} %add_add_fusion.17, s32[512]{0:T(512)S(1)} %add_add_fusion.18), kind=kLoop, calls=%fused_computation.55.clone.1 | loop fusion | flops 18874368 | bytes 6305792 | tf_op jit(solution)/shard_map/convert.4
  604.8 26.3 %cosine_convert_fusion.8 = (bf16[512,3072]{1,0:T(8,128)(2,1)S(1)}, bf16[512,3072]{1,0:T(8,128)(2,1)S(1)}) fusion(s32[3072]{0:T(1024)S(1)} %add_add_fusion.17, s32[512]{0:T(512)S(1)} %add_add_fusion.18), kind=kLoop, calls=%fused_computation.55.clone.1 | loop fusion | flops 18874368 | bytes 6305792 | tf_op jit(solution)/shard_map/convert.4
  635.0 26.3 %cosine_convert_fusion.8 = (bf16[512,3072]{1,0:T(8,128)(2,1)S(1)}, bf16[512,3072]{1,0:T(8,128)(2,1)S(1)}) fusion(s32[3072]{0:T(1024)S(1)} %add_add_fusion.17, s32[512]{0:T(512)S(1)} %add_add_fusion.18), kind=kLoop, calls=%fused_computation.55.clone.1 | loop fusion | flops 18874368 | bytes 6305792 | tf_op jit(solution)/shard_map/convert.4
  667.0 12.0 %add_convert_fusion.2 = (bf16[256,1,3072]{2,1,0:T(2,128)(2,1)S(1)}, bf16[256,1,3072]{2,1,0:T(2,128)(2,1)S(1)}) fusion(f32[256,2,3072]{2,1,0:T(2,128)S(1)} %fusion.64, f32[256,2,3072]{2,1,0:T(2,128)} %fusion.63), kind=kLoop, calls=%fused_computation.87 | loop fusion | flops 6291456 | bytes 15728640 | tf_op jit(solution)/shard_map/convert.17
  689.8 11.1 %reduce-scatter.8.cloned.1.call-done = f32[1024,256]{1,0:T(8,128)} async-done(((f32[2048,256]{1,0:T(8,128)}), f32[1024,256]{1,0:T(8,128)}) %reduce-scatter.8.cloned.1.call-update) | async-done | bytes 1048592 | tf_op jit(solution)/shard_map/reduce_scatter | solution.py:77
  709.6 117.7 %while.39 = (s32[]{:T(128)}, f32[4,512,256]{2,1,0:T(8,128)S(1)}, s32[4]{0:T(128)S(1)}, bf16[256,6144]{1,0:T(8,128)(2,1)}, s32[]{:T(128)}, /*index=5*/s32[]{:T(128)}) while((s32[]{:T(128)}, f32[4,512,256]{2,1,0:T(8,128)S(1)}, s32[4]{0:T(128)S(1)}, bf16[256,6144]{1,0:T(8,128)(2,1)}, s32[]{:T(128)}, /*index=5*/s32[]{:T(128)}) %tuple.133), condition=%wide.region_1.3_spmd.clone, body=%wide.region_0.0_spmd.clone.sunk | while | flops 1642208256 | bytes 28864632 | solution.py:78
  710.9 26.3 %cosine_convert_fusion.6 = (bf16[512,3072]{1,0:T(8,128)(2,1)S(1)}, bf16[512,3072]{1,0:T(8,128)(2,1)S(1)}) fusion(s32[3072]{0:T(1024)S(1)} %add_add_fusion.13, s32[512]{0:T(512)S(1)} %add_add_fusion.14), kind=kLoop, calls=%fused_computation.17.clone.1 | loop fusion | flops 18874368 | bytes 6305792 | tf_op jit(solution)/shard_map/convert
  740.3 26.3 %cosine_convert_fusion.6 = (bf16[512,3072]{1,0:T(8,128)(2,1)S(1)}, bf16[512,3072]{1,0:T(8,128)(2,1)S(1)}) fusion(s32[3072]{0:T(1024)S(1)} %add_add_fusion.13, s32[512]{0:T(512)S(1)} %add_add_fusion.14), kind=kLoop, calls=%fused_computation.17.clone.1 | loop fusion | flops 18874368 | bytes 6305792 | tf_op jit(solution)/shard_map/convert
  769.7 26.3 %cosine_convert_fusion.6 = (bf16[512,3072]{1,0:T(8,128)(2,1)S(1)}, bf16[512,3072]{1,0:T(8,128)(2,1)S(1)}) fusion(s32[3072]{0:T(1024)S(1)} %add_add_fusion.13, s32[512]{0:T(512)S(1)} %add_add_fusion.14), kind=kLoop, calls=%fused_computation.17.clone.1 | loop fusion | flops 18874368 | bytes 6305792 | tf_op jit(solution)/shard_map/convert
  799.2 26.3 %cosine_convert_fusion.6 = (bf16[512,3072]{1,0:T(8,128)(2,1)S(1)}, bf16[512,3072]{1,0:T(8,128)(2,1)S(1)}) fusion(s32[3072]{0:T(1024)S(1)} %add_add_fusion.13, s32[512]{0:T(512)S(1)} %add_add_fusion.14), kind=kLoop, calls=%fused_computation.17.clone.1 | loop fusion | flops 18874368 | bytes 6305792 | tf_op jit(solution)/shard_map/convert
  830.8 32.4 %reduce-scatter.4.cloned.1.call-done = f32[1024,256]{1,0:T(8,128)} async-done(((f32[2048,256]{1,0:T(8,128)}), f32[1024,256]{1,0:T(8,128)}) %reduce-scatter.4.cloned.1.call-update) | async-done | bytes 1048592 | tf_op jit(solution)/shard_map/reduce_scatter | solution.py:77
  869.1 47.5 %collective-permute-done.3 = f32[1250,1024]{1,0:T(8,128)} collective-permute-done((f32[1250,1024]{1,0:T(8,128)}, f32[1250,1024]{1,0:T(8,128)}, u32[]{:S(2)}, u32[]{:S(2)}) %collective-permute-start.3) | collective-permute-done | bytes 5120032 | tf_op jit(solution)/shard_map/ppermute | solution.py:17
  916.6 9.4 add_add_fusion.6
  933.3 106.7 %all-reduce.2.cloned.1.call-done = f32[625,2,1024]{2,1,0:T(2,128)} async-done(((f32[625,2,1024]{2,1,0:T(2,128)}), f32[625,2,1024]{2,1,0:T(2,128)}) %all-reduce.2.cloned.1.call-update) | async-done | bytes 5120016 | tf_op jit(solution)/shard_map/psum | solution.py:99
  (166 shorter events, 124.1 us)
Async XLA Ops:
  6.5 677.5 %reduce-scatter.6.cloned.1.call-start = ((), (), s32[]{:S(2)}) async-start(), calls=%async_computation.4 | async-start | bytes 3145728 | tf_op jit(solution)/shard_map/reduce_scatter | solution.py:77
  6.5 335.9 %collective-permute-start = (bf16[625,2,3072]{2,1,0:T(2,128)(2,1)}, bf16[625,2,3072]{2,1,0:T(2,128)(2,1)}, u32[]{:S(2)}, u32[]{:S(2)}) collective-permute-start(bf16[625,2,3072]{2,1,0:T(2,128)(2,1)} %bitcast.79), channel_id=1, source_target_pairs={{8,0},{16,8},{24,16},{32,24},{40,32},{48,40},{56,48},{64,56},{72,6... | collective-permute-start | bytes 23040008 | tf_op jit(solution)/shard_map/ppermute | solution.py:17
  13.6 488.1 %collective-permute-start.2 = (bf16[625,2,3072]{2,1,0:T(2,128)(2,1)}, bf16[625,2,3072]{2,1,0:T(2,128)(2,1)}, u32[]{:S(2)}, u32[]{:S(2)}) collective-permute-start(bf16[625,2,3072]{2,1,0:T(2,128)(2,1)} %bitcast.80), channel_id=1, source_target_pairs={{16,0},{24,8},{32,16},{40,24},{48,32},{56,40},{64,48},{72,56},{80,... | collective-permute-start | bytes 23040008 | tf_op jit(solution)/shard_map/ppermute | solution.py:17
  85.0 5.5 copy-start.1
  90.5 5.5 copy-start.2
  342.4 24.1 %slice-start.2 = ((s8[6291456]{0:T(1024)(128)(4,1)}), s8[2097152]{0:T(1024)(128)(4,1)S(1)}, s32[]{:S(2)}) async-start(s8[6291456]{0:T(1024)(128)(4,1)} %bitcast.77), calls=%async_computation.9 | async-start | bytes 4194304
  358.9 7.6 slice-start.3
  383.3 26.3 %copy-start.8 = (bf16[256,6144]{1,0:T(8,128)(2,1)S(1)}, bf16[256,6144]{1,0:T(8,128)(2,1)}, u32[]{:S(2)}) copy-start(bf16[256,6144]{1,0:T(8,128)(2,1)} %get-tuple-element.467) | copy-start | bytes 9437188 | tf_op jit(solution)/shard_map/while
  412.8 26.3 %copy-start.8 = (bf16[256,6144]{1,0:T(8,128)(2,1)S(1)}, bf16[256,6144]{1,0:T(8,128)(2,1)}, u32[]{:S(2)}) copy-start(bf16[256,6144]{1,0:T(8,128)(2,1)} %get-tuple-element.467) | copy-start | bytes 9437188 | tf_op jit(solution)/shard_map/while
  442.4 26.3 %copy-start.8 = (bf16[256,6144]{1,0:T(8,128)(2,1)S(1)}, bf16[256,6144]{1,0:T(8,128)(2,1)}, u32[]{:S(2)}) copy-start(bf16[256,6144]{1,0:T(8,128)(2,1)} %get-tuple-element.467) | copy-start | bytes 9437188 | tf_op jit(solution)/shard_map/while
  471.9 26.3 %copy-start.8 = (bf16[256,6144]{1,0:T(8,128)(2,1)S(1)}, bf16[256,6144]{1,0:T(8,128)(2,1)}, u32[]{:S(2)}) copy-start(bf16[256,6144]{1,0:T(8,128)(2,1)} %get-tuple-element.467) | copy-start | bytes 9437188 | tf_op jit(solution)/shard_map/while
  501.6 199.4 %reduce-scatter.8.cloned.1.call-start = ((), (), s32[]{:S(2)}) async-start(), calls=%async_computation.5 | async-start | bytes 3145728 | tf_op jit(solution)/shard_map/reduce_scatter | solution.py:77
  501.7 24.3 %slice-start = ((s8[6291456]{0:T(1024)(128)(4,1)}), s8[2097152]{0:T(1024)(128)(4,1)S(1)}, s32[]{:S(2)}) async-start(s8[6291456]{0:T(1024)(128)(4,1)} %bitcast.75), calls=%async_computation.7 | async-start | bytes 4194304
  518.4 7.6 slice-start.1
  542.8 121.3 %copy-start = (bf16[256,2,3072]{2,1,0:T(2,128)(2,1)S(1)}, bf16[256,2,3072]{2,1,0:T(2,128)(2,1)}, u32[]{:S(2)}) copy-start(bf16[256,2,3072]{2,1,0:T(2,128)(2,1)} %gather_fusion.1) | copy-start | bytes 9437188
  544.4 26.3 %copy-start.9 = (bf16[256,6144]{1,0:T(8,128)(2,1)S(1)}, bf16[256,6144]{1,0:T(8,128)(2,1)}, u32[]{:S(2)}) copy-start(bf16[256,6144]{1,0:T(8,128)(2,1)} %get-tuple-element.449) | copy-start | bytes 9437188 | tf_op jit(solution)/shard_map/while
  574.6 26.3 %copy-start.9 = (bf16[256,6144]{1,0:T(8,128)(2,1)S(1)}, bf16[256,6144]{1,0:T(8,128)(2,1)}, u32[]{:S(2)}) copy-start(bf16[256,6144]{1,0:T(8,128)(2,1)} %get-tuple-element.449) | copy-start | bytes 9437188 | tf_op jit(solution)/shard_map/while
  604.8 26.3 %copy-start.9 = (bf16[256,6144]{1,0:T(8,128)(2,1)S(1)}, bf16[256,6144]{1,0:T(8,128)(2,1)}, u32[]{:S(2)}) copy-start(bf16[256,6144]{1,0:T(8,128)(2,1)} %get-tuple-element.449) | copy-start | bytes 9437188 | tf_op jit(solution)/shard_map/while
  635.0 26.3 %copy-start.9 = (bf16[256,6144]{1,0:T(8,128)(2,1)S(1)}, bf16[256,6144]{1,0:T(8,128)(2,1)}, u32[]{:S(2)}) copy-start(bf16[256,6144]{1,0:T(8,128)(2,1)} %get-tuple-element.449) | copy-start | bytes 9437188 | tf_op jit(solution)/shard_map/while
  664.0 199.2 %reduce-scatter.4.cloned.1.call-start = ((), (), s32[]{:S(2)}) async-start(), calls=%async_computation.3 | async-start | bytes 3145728 | tf_op jit(solution)/shard_map/reduce_scatter | solution.py:77
  689.8 179.3 %collective-permute-start.1 = (f32[1250,1024]{1,0:T(8,128)}, f32[1250,1024]{1,0:T(8,128)}, u32[]{:S(2)}, u32[]{:S(2)}) collective-permute-start(f32[1250,1024]{1,0:T(8,128)} %fusion.75), channel_id=1, source_target_pairs={{120,0},{0,8},{8,16},{16,24},{24,32},{32,40},{40,48},{48,56},{56,6... | collective-permute-start | bytes 15360008 | tf_op jit(solution)/shard_map/ppermute | solution.py:17
  706.7 209.9 %collective-permute-start.3 = (f32[1250,1024]{1,0:T(8,128)}, f32[1250,1024]{1,0:T(8,128)}, u32[]{:S(2)}, u32[]{:S(2)}) collective-permute-start(f32[1250,1024]{1,0:T(8,128)} %fusion.81), channel_id=1, source_target_pairs={{112,0},{120,8},{0,16},{8,24},{16,32},{24,40},{32,48},{40,56},{48,... | collective-permute-start | bytes 15360008 | tf_op jit(solution)/shard_map/ppermute | solution.py:17
  709.6 120.0 %copy-start.13 = (pred[256]{0:T(512)(128)(4,1)S(1)}, pred[256]{0:T(512)(128)(4,1)}, u32[]{:S(2)}) copy-start(pred[256]{0:T(512)(128)(4,1)} %get-tuple-element.249) | copy-start | bytes 772
  709.6 120.0 %copy-start.14 = (pred[256]{0:T(512)(128)(4,1)S(1)}, pred[256]{0:T(512)(128)(4,1)}, u32[]{:S(2)}) copy-start(pred[256]{0:T(512)(128)(4,1)} %get-tuple-element.253) | copy-start | bytes 772
  709.6 153.6 %copy-start.11 = (s32[256]{0:T(256)S(1)}, s32[256]{0:T(256)}, u32[]{:S(2)}) copy-start(s32[256]{0:T(256)} %get-tuple-element.312) | copy-start | bytes 3076
  710.9 26.3 %copy-start.7 = (bf16[256,6144]{1,0:T(8,128)(2,1)S(1)}, bf16[256,6144]{1,0:T(8,128)(2,1)}, u32[]{:S(2)}) copy-start(bf16[256,6144]{1,0:T(8,128)(2,1)} %get-tuple-element.485) | copy-start | bytes 9437188 | tf_op jit(solution)/shard_map/while
  740.3 26.3 %copy-start.7 = (bf16[256,6144]{1,0:T(8,128)(2,1)S(1)}, bf16[256,6144]{1,0:T(8,128)(2,1)}, u32[]{:S(2)}) copy-start(bf16[256,6144]{1,0:T(8,128)(2,1)} %get-tuple-element.485) | copy-start | bytes 9437188 | tf_op jit(solution)/shard_map/while
  769.7 26.3 %copy-start.7 = (bf16[256,6144]{1,0:T(8,128)(2,1)S(1)}, bf16[256,6144]{1,0:T(8,128)(2,1)}, u32[]{:S(2)}) copy-start(bf16[256,6144]{1,0:T(8,128)(2,1)} %get-tuple-element.485) | copy-start | bytes 9437188 | tf_op jit(solution)/shard_map/while
  799.2 26.3 %copy-start.7 = (bf16[256,6144]{1,0:T(8,128)(2,1)S(1)}, bf16[256,6144]{1,0:T(8,128)(2,1)}, u32[]{:S(2)}) copy-start(bf16[256,6144]{1,0:T(8,128)(2,1)} %get-tuple-element.485) | copy-start | bytes 9437188 | tf_op jit(solution)/shard_map/while
  828.7 211.3 %all-reduce.2.cloned.1.call-start = ((), (), s32[]{:S(2)}) async-start(), calls=%async_computation.6 | async-start | bytes 10240000 | tf_op jit(solution)/shard_map/psum | solution.py:99
  866.8 49.8 %copy-start.5 = (f32[1024,256]{1,0:T(8,128)S(1)}, f32[1024,256]{1,0:T(8,128)}, u32[]{:S(2)}) copy-start(f32[1024,256]{1,0:T(8,128)} %reduce-scatter.6.cloned.1.call-done) | copy-start | bytes 3145732
  866.9 49.8 %copy-start.12 = (s32[256]{0:T(256)S(1)}, s32[256]{0:T(256)}, u32[]{:S(2)}) copy-start(s32[256]{0:T(256)} %get-tuple-element.308) | copy-start | bytes 3076
  (5 other events, 10.6 us)
Sparse Core Ops, SparseCore 0:
  501.7 36.7 reduce-scatter.5
  664.2 36.7 reduce-scatter.7
  828.8 34.3 reduce-scatter.3
  933.5 106.5 all-reduce.1
where the time goes:
time: 1060 us; the launch traced here: 1050 us
  waiting for transfers between devices  439 us (41%)
  other arithmetic  407 us (38%)
  local copies, waits for them, and re-layouts  131 us (12%)
  matrix products  51.9 us (5%)
  between operations  13.9 us (1%)
    another operation x15, other arithmetic  353 us
    ppermute x4, waiting for transfers between devices, shifted(): return lax.ppermute(block, axis, route)  288 us
    psum x1, waiting for transfers between devices, per_device(): local_stack = lax.psum(local_stack, 'seg')  107 us
    gather x3, local copies, waits for them, and re-layouts, per_device(): first = jnp.take(own_block, first_index, axis=0).astype(jnp.float32)  49.2 us
    reduce_scatter x3, waiting for transfers between devices, per_device(): lax.psum_scatter(lax.map(one_block, offsets).reshape(lax.axis_size('lag')...  43.5 us
    gather x2, local copies, waits for them, and re-layouts, per_device(): second = jnp.take(partner_block, second_index, axis=0).astype(jnp.float32)  33.3 us
    dot_general x5, matrix products, bin_rows(): lax.dot_general(selector, corr, (((1,), (1,)), ((), ())), precision=lax.P...  26.8 us
    dot_general x12, matrix products, one_block(): lax.dot_general(table, cross, (((1,), (1,)), ((), ())), preferred_element...  25.1 us
  transfers between devices with their start and end apart: 8, of which 5 were waited for; matrix products, arithmetic and copies ran while one was open for 53% of the time, Pallas kernels for 0%

commit v1 on v0

v1 whole, which is shorter than its diff:
```python
import functools
import math

import jax
import jax.numpy as jnp
from jax import lax
from jax.experimental import pallas as pl
from jax.experimental.pallas import tpu as pltpu
from jax.sharding import PartitionSpec as P

FREQ = 6144
LAGS = 2048
BINS = 2
HALF = 128
QUARTER = LAGS // 4
TILE = 512
PICK_MB = 20
CORR_MB = 56
F32 = jnp.float32
BF16 = jnp.bfloat16


def route(axis, move):
    return [(i, move(i)) for i in range(lax.axis_size(axis))]


def shifted(value, distance):
    count = lax.axis_size("chan")
    return lax.ppermute(value, "chan", route("chan", lambda i: (i + distance) % count))


def swapped(value, axis, bit):
    return lax.ppermute(value, axis, route(axis, lambda i: i ^ bit))


def params(megabytes=32):
    return pltpu.CompilerParams(vmem_limit_bytes=megabytes << 20)


def dot(a, b):
    return jnp.dot(a, b, preferred_element_type=F32)


def cost(flops, moved):
    return pl.CostEstimate(flops=flops, bytes_accessed=moved, transcendentals=0)


def pick_kernel(index_ref, rows_ref, *refs):
    outs, hot_ref = refs[:-1], refs[-1]

    @pl.when(pl.program_id(0) == 0)
    def _():
        ids = lax.broadcasted_iota(jnp.int32, hot_ref.shape, 1)
        hot_ref[...] = jnp.where(index_ref[...] == ids, 1.0, 0.0).astype(BF16)

    for part in range(2):
        picked = dot(hot_ref[...], rows_ref[part]).astype(BF16)
        row = 0
        for out_ref in outs:
            count = out_ref.shape[1]
            out_ref[part] = picked[row : row + count]
            row += count


def pick(groups, rows):
    counts = [sum(index.shape[0] for index in group) for group in groups]
    index = jnp.concatenate([index for group in groups for index in group])
    (total,), (_, chans, freqs) = index.shape, rows.shape
    return pl.pallas_call(
        pick_kernel,
        out_shape=[jax.ShapeDtypeStruct((2, count, freqs), BF16) for count in counts],
        grid=(freqs // TILE,),
        in_specs=[
            pl.BlockSpec((total, 1), lambda i: (0, 0)),
            pl.BlockSpec((2, chans, TILE), lambda i: (0, 0, i)),
        ],
        out_specs=[pl.BlockSpec((2, count, TILE), lambda i: (0, 0, i)) for count in counts],
        scratch_shapes=[pltpu.VMEM((total, chans), BF16)],
        compiler_params=params(PICK_MB),
        cost_estimate=cost(4 * total * chans * freqs, 4 * (chans + total) * freqs),
        name="pick",
    )(index[:, None], rows)


def table_kernel(coarse_ref, fine_ref, sign_ref, out_ref):
    cos_b, sin_b = fine_ref[0], fine_ref[1]
    width = cos_b.shape[1]
    for step in range(2 * QUARTER // width):
        cos_a, sin_a = coarse_ref[0, :, step : step + 1], coarse_ref[1, :, step : step + 1]
        cols = slice(step * width, (step + 1) * width)
        out_ref[0, :, cols] = (cos_a * cos_b - sin_a * sin_b).astype(BF16)
        out_ref[1, :, cols] = (sign_ref[0] * (sin_a * cos_b + cos_a * sin_b)).astype(BF16)


def lag_table(freq_index, core, sign):
    freqs, width = freq_index.shape[0], 128
    steps = 2 * QUARTER // width
    step = jnp.arange(steps, dtype=jnp.int32)
    start = (core ^ (step // (steps // 2))) * QUARTER + (step % (steps // 2)) * width

    def waves(doubled, freq):
        angle = jnp.mod(doubled * freq, 4 * FREQ).astype(F32) * (math.pi / (2 * FREQ))
        return jnp.stack([jnp.cos(angle), jnp.sin(angle)])

    coarse = waves(2 * start[:, None], freq_index[None, :]).transpose(0, 2, 1)
    odd = 2 * jnp.arange(width, dtype=jnp.int32) + 1
    fine = waves(odd[None, :], freq_index[:, None])
    return pl.pallas_call(
        table_kernel,
        out_shape=jax.ShapeDtypeStruct((2, freqs, 2 * QUARTER), BF16),
        grid=(freqs // TILE,),
        in_specs=[
            pl.BlockSpec((2, TILE, steps), lambda i: (0, i, 0)),
            pl.BlockSpec((2, TILE, width), lambda i: (0, i, 0)),
            pl.BlockSpec(memory_space=pltpu.SMEM),
        ],
        out_specs=pl.BlockSpec((2, TILE, 2 * QUARTER), lambda i: (0, i, 0)),
        compiler_params=params(),
        cost_estimate=cost(12 * freqs * LAGS, 4 * freqs * LAGS),
        name="table",
    )(coarse, fine, sign[None])


def corr_kernel(count, *refs):
    firsts, seconds = refs[:count], refs[count : 2 * count]
    turn_ref, table_ref, keep_ref, send_ref, cos_acc, sin_acc = refs[2 * count :]
    step = pl.program_id(0)

    @pl.when(step == 0)
    def _():
        cos_acc[...] = jnp.zeros_like(cos_acc)
        sin_acc[...] = jnp.zeros_like(sin_acc)

    turn_cos, turn_sin = turn_ref[0:1], turn_ref[1:2]
    row = 0
    for first_ref, second_ref in zip(firsts, seconds):
        first_re, first_im = first_ref[0].astype(F32), first_ref[1].astype(F32)
        second_re, second_im = second_ref[0].astype(F32), second_ref[1].astype(F32)
        real = first_re * second_re + first_im * second_im
        imag = first_im * second_re - first_re * second_im
        turned_re = (real * turn_cos + imag * turn_sin).astype(BF16)
        turned_im = (imag * turn_cos - real * turn_sin).astype(BF16)
        here = slice(row, row + first_ref.shape[1])
        cos_acc[here] += dot(turned_re, table_ref[0])
        sin_acc[here] += dot(turned_im, table_ref[1])
        row += first_ref.shape[1]

    @pl.when(step == pl.num_programs(0) - 1)
    def _():
        scale = FREQ ** (-0.5)
        total = (cos_acc[...] + sin_acc[...]) * scale
        other = (cos_acc[...] - sin_acc[...]) * scale
        keep_ref[0] = total[:, :QUARTER]
        keep_ref[1] = other[:, :QUARTER]
        send_ref[0] = total[:, QUARTER:].astype(BF16)
        send_ref[1] = other[:, QUARTER:].astype(BF16)


def correlate(pairs, turn, table):
    firsts, seconds = zip(*pairs)
    rows = sum(count for _, count, _ in firsts)
    freqs = table.shape[1]

    def spec(value):
        _, count, place = value
        return pl.BlockSpec((2, count, TILE), lambda i: (0, place, i))

    flat = firsts + seconds
    return pl.pallas_call(
        functools.partial(corr_kernel, len(pairs)),
        out_shape=(
            jax.ShapeDtypeStruct((2, rows, QUARTER), F32),
            jax.ShapeDtypeStruct((2, rows, QUARTER), BF16),
        ),
        grid=(freqs // TILE,),
        in_specs=[spec(value) for value in flat]
        + [
            pl.BlockSpec((2, TILE), lambda i: (0, i)),
            pl.BlockSpec((2, TILE, 2 * QUARTER), lambda i: (0, i, 0)),
        ],
        out_specs=(
            pl.BlockSpec((2, rows, QUARTER), lambda i: (0, 0, 0)),
            pl.BlockSpec((2, rows, QUARTER), lambda i: (0, 0, 0)),
        ),
        scratch_shapes=[pltpu.VMEM((rows, 2 * QUARTER), F32)] * 2,
        compiler_params=params(CORR_MB),
        cost_estimate=cost(4 * rows * freqs * LAGS, 4 * freqs * LAGS + 16 * rows * freqs),
        name="corr",
    )(*[value[0] for value in flat], turn, table)


def fold_kernel(keep_ref, other_ref, mine_ref, far_ref):
    mine_ref[...] = (keep_ref[0] + other_ref[0].astype(F32)).astype(BF16)
    far_ref[...] = (keep_ref[1] + other_ref[1].astype(F32)).astype(BF16)


def fold(keep, other):
    shape = jax.ShapeDtypeStruct(keep.shape[1:], BF16)
    return pl.pallas_call(
        fold_kernel, out_shape=(shape, shape), compiler_params=params(), name="fold"
    )(keep, other)


def sum_kernel(flip_ref, mine_ref, near_ref, far_ref, across_ref, out_ref):
    total = (mine_ref[...].astype(F32) + near_ref[...].astype(F32)) + (
        far_ref[...].astype(F32) + across_ref[...].astype(F32)
    )
    total = total.astype(BF16)
    size = total.shape[1]
    row = lax.broadcasted_iota(jnp.int32, (size, size), 0)
    col = lax.broadcasted_iota(jnp.int32, (size, size), 1)
    wanted = jnp.where(flip_ref[0] == 1, size - 1 - col, col)
    order = jnp.where(row == wanted, 1.0, 0.0).astype(BF16)
    out_ref[...] = dot(total, order).astype(BF16)


def reduced(partial, flip):
    keep, send = partial
    mine, far = fold(keep, swapped(send, "seg", 1))
    near = swapped(far, "lag", 1)
    opposite = swapped(mine, "seg", 2)
    seg, lag = lax.axis_size("seg"), lax.axis_size("lag")
    pairs = [(s * lag + g, (s ^ 2) * lag + (g ^ 1)) for s in range(seg) for g in range(lag)]
    across = lax.ppermute(far, ("seg", "lag"), pairs)
    vmem = pl.BlockSpec(memory_space=pltpu.VMEM)
    return pl.pallas_call(
        sum_kernel,
        out_shape=jax.ShapeDtypeStruct(mine.shape, BF16),
        in_specs=[pl.BlockSpec(memory_space=pltpu.SMEM)] + [vmem] * 4,
        compiler_params=params(),
        name="sum4",
    )(flip[None], mine, near, opposite, across)


def final_kernel(at_ref, ids_ref, early_ref, early2_ref, late_ref, late2_ref, out_ref):
    chans = out_ref.shape[0]
    base = pl.program_id(0) * chans
    early = early_ref.shape[0]
    slots = ids_ref.shape[1]
    for bin_index in range(BINS):
        chan = base + lax.broadcasted_iota(jnp.int32, (chans, slots), 0)
        hot = jnp.where(ids_ref[...] == chan * BINS + bin_index, 1.0, 0.0).astype(BF16)
        mine = dot(hot[:, :early], early_ref[...]) + dot(hot[:, early:], late_ref[...])
        other = dot(hot[:, :early], early2_ref[...]) + dot(hot[:, early:], late2_ref[...])
        low = at_ref[0] == 0
        out_ref[:, bin_index, :QUARTER] = jnp.where(low, mine, other)
        out_ref[:, bin_index, QUARTER:] = jnp.where(low, other, mine)


def final(at, ids, early, early2, late, late2, chans):
    tile = 128
    whole = [pl.BlockSpec(v.shape, lambda i: (0, 0)) for v in (ids, early, early2, late, late2)]
    return pl.pallas_call(
        final_kernel,
        out_shape=jax.ShapeDtypeStruct((chans, BINS, LAGS // 2), F32),
        grid=(pl.cdiv(chans, tile),),
        in_specs=[pl.BlockSpec(memory_space=pltpu.SMEM)] + whole,
        out_specs=pl.BlockSpec((tile, BINS, LAGS // 2), lambda i: (i, 0, 0)),
        compiler_params=params(48),
        name="final",
    )(at[None], ids, early, early2, late, late2)


def per_device(spectra, pair_local, pair_partner, pair_bin, pair_owner, pair_count):
    block = lax.axis_index("chan")
    blocks = lax.axis_size("chan")
    lag_index = lax.axis_index("lag")
    core = lax.axis_index("seg") % 2
    own = spectra[0]
    chans, _, half_freq = own.shape
    slots = pair_local.shape[2]
    rows = own.transpose(1, 0, 2)
    before, before2 = (block - 1) % blocks, (block - 2) % blocks

    first_up = [pair_local[block, 1, HALF:], pair_local[block, 2, :HALF]]
    first_down = [pair_partner[before, 1, :HALF], pair_partner[before2, 2, :HALF]]
    last_up, last_down = pair_local[block, 2, HALF:], pair_partner[before2, 2, HALF:]
    picked = pick([first_up, first_down], rows)
    picked, rows, zero = lax.optimization_barrier((picked, rows, jnp.int32(0)))
    from_before, from_after = [shifted(picked[0], 1)], [shifted(picked[1], -1)]

    freq_index = lag_index * half_freq + jnp.arange(half_freq, dtype=jnp.int32) + 1 + zero
    sign = jnp.where(lag_index == 0, 1.0, -1.0).astype(F32)
    table = lag_table(freq_index, core, sign)
    angle = freq_index.astype(F32) * (math.pi / (2 * FREQ))
    turn = jnp.stack([jnp.cos(angle), jnp.sin(angle)])

    (local,) = pick(
        [
            [
                pair_local[block, 0] + zero,
                pair_partner[block, 0],
                pair_local[block, 1, :HALF],
                pair_partner[before, 1, HALF:],
            ]
        ],
        rows,
    )
    flip = 1 - lag_index

    def at(value, count, place):
        return value, count, place

    def total(pairs):
        return reduced(correlate(pairs, turn, table), flip)

    partial0 = correlate([(at(local, slots, 0), at(local, slots, 1))], turn, table)
    partial0, last_up, last_down = lax.optimization_barrier((partial0, last_up, last_down))
    picked = pick([[last_up], [last_down]], rows)
    from_before.append(shifted(picked[0], 1))
    from_after.append(shifted(picked[1], -1))
    corr0 = reduced(partial0, flip)
    corr1 = total(
        [
            (at(local, HALF, 4), at(from_after[0], HALF, 0)),
            (at(from_before[0], HALF, 0), at(local, HALF, 5)),
            (at(from_before[0], HALF, 1), at(from_after[0], HALF, 1)),
        ]
    )
    corr2 = total([(at(from_before[1], HALF, 0), at(from_after[1], HALF, 0))])
    to_after = jnp.concatenate([corr1[:HALF], corr1[2 * HALF :]])
    to_before = corr1[HALF:]
    early = jnp.concatenate(
        [corr0, corr1[: 2 * HALF], shifted(to_after, 1), shifted(to_before, -1)]
    )
    late = jnp.concatenate([shifted(corr2, 1), shifted(corr2, -1)])

    slot_ids = jnp.arange(slots, dtype=jnp.int32)

    def targets(source, round_index, owner):
        index = pair_local if owner == 0 else pair_partner
        live = slot_ids < pair_count[source, round_index]
        hit = live & (pair_owner[source, round_index] == owner)
        row = index[source, round_index] * BINS + pair_bin[source, round_index]
        return jnp.where(hit, row, -1)

    live0 = slot_ids < pair_count[block, 0]
    chan0 = jnp.where(pair_owner[block, 0] == 0, pair_local[block, 0], pair_partner[block, 0])
    row0 = jnp.where(live0, chan0 * BINS + pair_bin[block, 0], -1)
    near0, near1 = targets(block, 1, 0), targets(before, 1, 1)
    far0, far1 = targets(block, 2, 0), targets(before2, 2, 1)
    ids = jnp.concatenate(
        [
            row0,
            near0[:HALF],
            near1[HALF:],
            near1[:HALF],
            far1[:HALF],
            near0[HALF:],
            far0[:HALF],
            far1[HALF:],
            far0[HALF:],
        ]
    )[None, :]
    place = core ^ flip
    return final(
        place, ids, early, swapped(early, "seg", 1), late, swapped(late, "seg", 1), chans
    )


def solution(mesh):
    return jax.shard_map(
        per_device,
        mesh=mesh,
        in_specs=(P("seg", "chan", None, "lag"), P(), P(), P(), P(), P()),
        out_specs=P("chan", None, "lag"),
        check_vma=False,
    )
```

time: 1060 us -> 181 us (0.17)
  waiting for transfers between devices: 439 us -> 23.3 us
  other arithmetic: 407 us -> 19.3 us
  local copies, waits for them, and re-layouts: 131 us -> 22.8 us
  Pallas kernels: 0 us -> 74.4 us
  matrix products: 51.9 us -> 0 us
  starting transfers between devices: 10.5 us -> 40.6 us
  between operations: 13.9 us -> 0.52 us
    another operation x15 -> x3, other arithmetic: 353 us -> 3.55 us  [the longest x2 2.93 us: waves(): return jnp.stack([jnp.cos(angle), jnp.sin(angle)])]
    ppermute x4 -> x22, waiting for transfers between devices: 288 us -> 23.3 us  [the longest x8 22.2 us: shifted(): lax.ppermute(value, 'chan', route('chan', lambda i: (i + distance) % count))]
    psum x1 -> x0, waiting for transfers between devices: 107 us -> none  [per_device(): local_stack = lax.psum(local_stack, 'seg')]
    gather x6 -> x0, local copies, waits for them, and re-layouts: 98.9 us -> none  [the longest x3 49.2 us: per_device(): first = jnp.take(own_block, first_index, axis=0).astype(jnp.float32)]
    pallas_call x0 -> x14, Pallas kernels: none -> 74.4 us  [the longest x3 34.2 us: correlate(): pl.pallas_call(functools.partial(corr_kernel, len(pairs)), out_shape=(jax...]
    dot_general x17 -> x0, matrix products: 51.9 us -> none  [the longest x5 26.8 us: bin_rows(): lax.dot_general(selector, corr, (((1,), (1,)), ((), ())), precision=lax.P...]
    reduce_scatter x3 -> x0, waiting for transfers between devices: 43.5 us -> none  [per_device(): lax.psum_scatter(lax.map(one_block, offsets).reshape(lax.axis_size('lag')...]
    convert_element_type x6 -> x0, other arithmetic: 34.6 us -> none  [the longest x3 16.6 us: per_device(): first = jnp.take(own_block, first_index, axis=0).astype(jnp.float32)]
  transfers between devices with their start and end apart: 8 -> 22, of which waited for: 5 -> 5; matrix products, arithmetic and copies ran while one was open for 53% -> 12% of each run, Pallas kernels for 0% -> 33%
where the time goes in v1:
time: 181 us
  Pallas kernels  74.4 us (41%)
  starting transfers between devices  40.6 us (22%)
  waiting for transfers between devices  23.3 us (13%)
  local copies, waits for them, and re-layouts  22.8 us (13%)
  other arithmetic  19.3 us (11%)
    pallas_call x3, Pallas kernels, correlate(): pl.pallas_call(functools.partial(corr_kernel, len(pairs)), out_shape=(jax...  34.2 us
    pallas_call x3, Pallas kernels, pick(): pl.pallas_call(pick_kernel, out_shape=[jax.ShapeDtypeStruct((2, count, fr...  23.1 us
    ppermute x8, waiting for transfers between devices, shifted(): lax.ppermute(value, 'chan', route('chan', lambda i: (i + distance) % count))  22.2 us
    ppermute x8, starting transfers between devices, shifted(): lax.ppermute(value, 'chan', route('chan', lambda i: (i + distance) % count))  18.4 us
    unnamed x59, local copies, waits for them, and re-layouts  18.4 us
    ppermute x11, starting transfers between devices, swapped(): return lax.ppermute(value, axis, route(axis, lambda i: i ^ bit))  16.9 us
    pallas_call x1, Pallas kernels, lag_table(): pl.pallas_call(table_kernel, out_shape=jax.ShapeDtypeStruct((2, freqs, 2...  9.47 us
    cos x2, other arithmetic, waves(): return jnp.stack([jnp.cos(angle), jnp.sin(angle)])  8.6 us
  transfers between devices with their start and end apart: 22, of which 5 were waited for; matrix products, arithmetic and copies ran while one was open for 12% of the time, Pallas kernels for 33%

profile of v1, /device:TPU:1, one launch (start us, length us, event | category | flops | bytes accessed | tf_op | source)
XLA Modules:
  0.0 180.9 jit_solution(3618372136735553674)
XLA Ops:
  1.5 5.5 %copy.18 = bf16[1,625,2,3072]{3,1,2,0:T(8,128)(2,1)S(1)} copy(bf16[1,625,2,3072]{3,2,1,0:T(2,128)(2,1)} %param.6) | data formatting | bytes 15360000 | tf_op args[0]
  7.0 8.1 %pick.3 = (bf16[2,256,3072]{2,1,0:T(8,128)(2,1)}, bf16[2,256,3072]{2,1,0:T(8,128)(2,1)}) custom-call(s32[512,1]{1,0:T(8,128)S(1)} %copy.13.index_ref, bf16[2,625,3072]{2,1,0:T(8,128)(2,1)S(1)} %bitcast.39), custom_call_target="tpu_custom_call" | custom-call | flops 3932160000 | bytes 13971456 | tf_op jit(solution)/shard_map/pick/pallas_call | solution.py:69
  15.1 2.1 %collective-permute-start.4 = (bf16[2,256,3072]{2,1,0:T(8,128)(2,1)}, bf16[2,256,3072]{2,1,0:T(8,128)(2,1)}, u32[]{:S(2)}, u32[]{:S(2)}) collective-permute-start(bf16[2,256,3072]{2,1,0:T(8,128)(2,1)} %get-tuple-element.39), channel_id=1, source_target_pairs={{0,8},{8,16},{16,24},{24,32},{32,40},{40,48},{48,56},{56,64},{64,7... | collective-permute-start | bytes 9437192 | tf_op jit(solution)/shard_map/ppermute | solution.py:29
  17.3 4.9 %collective-permute-start.5 = (bf16[2,256,3072]{2,1,0:T(8,128)(2,1)}, bf16[2,256,3072]{2,1,0:T(8,128)(2,1)}, u32[]{:S(2)}, u32[]{:S(2)}) collective-permute-start(bf16[2,256,3072]{2,1,0:T(8,128)(2,1)} %get-tuple-element.40), channel_id=1, source_target_pairs={{0,120},{8,0},{16,8},{24,16},{32,24},{40,32},{48,40},{56,48},{64,5... | collective-permute-start | bytes 9437192 | tf_op jit(solution)/shard_map/ppermute | solution.py:29
  26.9 8.1 %fusion.5 = (f32[1,3072,128]{2,1,0:T(8,128)}, f32[1,3072,128]{2,1,0:T(8,128)}) fusion(s32[3072]{0:T(1024)S(1)} %add_add_fusion, s32[128]{0:T(128)S(1)} %multiply_add_fusion), kind=kLoop, calls=%fused_computation.9 | loop fusion | flops 3538944 | bytes 3158528 | tf_op jit(solution)/shard_map/cos | solution.py:103
  35.7 1.9 %copy.15 = f32[2,8,3072]{1,2,0:T(8,128)S(1)} copy(f32[2,8,3072]{2,1,0:T(8,128)} %pad_maximum_fusion.3) | data formatting | bytes 393216 | tf_op jit(solution)/shard_map/stack | solution.py:103
  37.6 2.2 %pad_maximum_fusion.fine_ref = f32[2,3072,128]{2,1,0:T(8,128)S(1)} fusion(f32[1,3072,128]{2,1,0:T(8,128)} %get-tuple-element.80, f32[1,3072,128]{2,1,0:T(8,128)} %get-tuple-element.79), kind=kLoop, calls=%fused_computation.1 | loop fusion | flops 786432 | bytes 6291456 | tf_op jit(solution)/shard_map/stack | solution.py:103
  39.8 9.5 %table.1.refs_3_.refs_7_ = bf16[2,3072,1024]{2,1,0:T(8,128)(2,1)S(1)} custom-call(f32[2,3072,8]{2,1,0:T(8,128)S(1)} %bitcast.44, f32[2,3072,128]{2,1,0:T(8,128)S(1)} %pad_maximum_fusion.fine_ref, f32[1]{0:T(128)} %bitcast.24.sign_ref), custom_call_target="tpu_custom_call" | custom-call | flops 75497472 | bytes 25165824 | tf_op jit(solution)/shard_map/table/pallas_call | solution.py:108
  49.3 4.6 %copy-done = bf16[2,3072,1024]{2,1,0:T(8,128)(2,1)} copy-done((bf16[2,3072,1024]{2,1,0:T(8,128)(2,1)}, bf16[2,3072,1024]{2,1,0:T(8,128)(2,1)S(1)}, u32[]{:S(2)}) %copy-start) | copy-done | bytes 12582936
  55.2 9.8 %pick.4.refs_0_.refs_1_.refs_4_ = bf16[2,768,3072]{2,1,0:T(8,128)(2,1)S(1)} custom-call(s32[768,1]{1,0:T(8,128)S(1)} %broadcast_in_dim.43.index_ref, bf16[2,625,3072]{2,1,0:T(8,128)(2,1)S(1)} %bitcast.42), custom_call_target="tpu_custom_call" | custom-call | flops 5898240000 | bytes 17117184 | tf_op jit(solution)/shard_map/pick/pallas_call | solution.py:69
  65.0 3.6 %copy-done.1 = bf16[2,768,3072]{2,1,0:T(8,128)(2,1)} copy-done((bf16[2,768,3072]{2,1,0:T(8,128)(2,1)}, bf16[2,768,3072]{2,1,0:T(8,128)(2,1)S(1)}, u32[]{:S(2)}) %copy-start.1) | copy-done | bytes 9437208
  68.6 11.2 %corr.3 = (f32[2,256,512]{2,1,0:T(8,128)}, bf16[2,256,512]{2,1,0:T(8,128)(2,1)}) custom-call(bf16[2,768,3072]{2,1,0:T(8,128)(2,1)} %copy-done.1, bf16[2,768,3072]{2,1,0:T(8,128)(2,1)} %copy-done.1, f32[2,3072]{1,0:T(2,128)} %pad_maximum_fusion.4.refs_2_.refs_6_, bf16[2,3072,1024]{2,1,0:T(8,128)(2,1)} %copy-done), custom_call_target="tpu_custom_call" | custom-call | flops 6442450944 | bytes 37748736 | tf_op jit(solution)/shard_map/corr/pallas_call | solution.py:169
  79.9 3.2 %copy-done.3 = bf16[1,625,2,3072]{3,1,2,0:T(8,128)(2,1)S(1)} copy-done((bf16[1,625,2,3072]{3,1,2,0:T(8,128)(2,1)S(1)}, bf16[1,625,2,3072]{3,1,2,0:T(8,128)(2,1)}, u32[]{:S(2)}) %copy-start.3) | copy-done | bytes 7680024
  83.1 5.2 %pick.5 = (bf16[2,128,3072]{2,1,0:T(8,128)(2,1)}, bf16[2,128,3072]{2,1,0:T(8,128)(2,1)}) custom-call(s32[256,1]{1,0:T(8,128)S(1)} %copy.16.index_ref, bf16[2,625,3072]{2,1,0:T(8,128)(2,1)S(1)} %bitcast.43), custom_call_target="tpu_custom_call" | custom-call | flops 1966080000 | bytes 10825728 | tf_op jit(solution)/shard_map/pick/pallas_call | solution.py:69
  88.4 5.0 %collective-permute-start.14 = (bf16[2,128,3072]{2,1,0:T(8,128)(2,1)}, bf16[2,128,3072]{2,1,0:T(8,128)(2,1)}, u32[]{:S(2)}, u32[]{:S(2)}) collective-permute-start(bf16[2,128,3072]{2,1,0:T(8,128)(2,1)} %get-tuple-element.48), channel_id=1, source_target_pairs={{0,120},{8,0},{16,8},{24,16},{32,24},{40,32},{48,40},{56,48},{64,5... | collective-permute-start | bytes 4718600 | tf_op jit(solution)/shard_map/ppermute | solution.py:29
  93.4 13.9 %corr.4 = (f32[2,384,512]{2,1,0:T(8,128)}, bf16[2,384,512]{2,1,0:T(8,128)(2,1)}) custom-call(bf16[2,768,3072]{2,1,0:T(8,128)(2,1)} %copy-done.1, bf16[2,256,3072]{2,1,0:T(8,128)(2,1)} %collective-permute-done.4.refs_1_.refs_2_, bf16[2,256,3072]{2,1,0:T(8,128)(2,1)} %collective-permute-done.4.refs_1_.refs_2_, ...), custom_call_target="tpu_custom_call" | custom-call | flops 9663676416 | bytes 44040192 | tf_op jit(solution)/shard_map/corr/pallas_call | solution.py:169
  107.4 1.5 collective-permute-start.6
  110.2 1.8 %and_select_fusion.2 = (s32[256]{0:T(256)}, s32[256]{0:T(256)}) fusion(s32[256]{0:T(256)S(1)} %bitcast.49, pred[256]{0:T(512)(128)(4,1)S(1)} %copy-done.10, s32[]{:T(128)} %bitcast.11, s32[256]{0:T(256)S(1)} %bitcast.50, pred[256]{0:T(512)(128)(4,1)S(1)} %copy-done.11, s32[]{:T(128)} %bitcast.9), kind=kLoop, calls=%fused_computation.77 | loop fusion | flops 1536 | bytes 4616 | tf_op jit(solution)/shard_map/jit(_where)/select_n | solution.py:335
  112.1 1.4 copy-done.4
  113.6 2.6 %collective-permute-start.9 = (bf16[384,512]{1,0:T(8,128)(2,1)S(1)}, bf16[384,512]{1,0:T(8,128)(2,1)S(1)}, u32[]{:S(2)}, u32[]{:S(2)}) collective-permute-start(bf16[384,512]{1,0:T(8,128)(2,1)S(1)} %get-tuple-element.44), channel_id=1, source_target_pairs={{0,5},{1,4},{2,7},{3,6},{4,1},{5,0},{6,3},{7,2},{8,13},{9,12},{10,... | collective-permute-start | bytes 1179656 | tf_op jit(solution)/shard_map/ppermute | solution.py:224
  117.7 9.2 %collective-permute-done.13.refs_0_ = bf16[2,128,3072]{2,1,0:T(8,128)(2,1)} collective-permute-done((bf16[2,128,3072]{2,1,0:T(8,128)(2,1)}, bf16[2,128,3072]{2,1,0:T(8,128)(2,1)}, u32[]{:S(2)}, u32[]{:S(2)}) %collective-permute-start.13) | collective-permute-done | bytes 1572896 | tf_op jit(solution)/shard_map/ppermute | solution.py:29
  126.9 2.5 %collective-permute-start.3 = (bf16[256,512]{1,0:T(8,128)(2,1)S(1)}, bf16[256,512]{1,0:T(8,128)(2,1)S(1)}, u32[]{:S(2)}, u32[]{:S(2)}) collective-permute-start(bf16[256,512]{1,0:T(8,128)(2,1)S(1)} %get-tuple-element.38), channel_id=1, source_target_pairs={{0,5},{1,4},{2,7},{3,6},{4,1},{5,0},{6,3},{7,2},{8,13},{9,12},{10,... | collective-permute-start | bytes 786440 | tf_op jit(solution)/shard_map/ppermute | solution.py:224
  129.4 9.1 %corr.5 = (f32[2,128,512]{2,1,0:T(8,128)}, bf16[2,128,512]{2,1,0:T(8,128)(2,1)}) custom-call(bf16[2,128,3072]{2,1,0:T(8,128)(2,1)} %collective-permute-done.13.refs_0_, bf16[2,128,3072]{2,1,0:T(8,128)(2,1)} %collective-permute-done.14.refs_1_, f32[2,3072]{1,0:T(2,128)} %pad_maximum_fusion.4.refs_2_.refs_6_, bf16[2,3072,1024]{2,1,0:T(8,128)(2,1)} %copy-done), custom_call_target="tpu_custom_call" | custom-call | flops 3221225472 | bytes 31457280 | tf_op jit(solution)/shard_map/corr/pallas_call | solution.py:169
  139.9 2.7 %collective-permute-start.15 = (bf16[2,128,512]{2,1,0:T(8,128)(2,1)}, bf16[2,128,512]{2,1,0:T(8,128)(2,1)S(1)}, u32[]{:S(2)}, u32[]{:S(2)}) collective-permute-start(bf16[2,128,512]{2,1,0:T(8,128)(2,1)} %get-tuple-element.50), channel_id=1, source_target_pairs={{0,2},{2,0},{4,6},{6,4},{1,3},{3,1},{5,7},{7,5},{8,10},{10,8},{12,... | collective-permute-start | bytes 786440 | tf_op jit(solution)/shard_map/ppermute | solution.py:33
  143.1 4.6 %collective-permute-start.11 = (bf16[256,512]{1,0:T(8,128)(2,1)S(1)}, bf16[256,512]{1,0:T(8,128)(2,1)S(1)}, u32[]{:S(2)}, u32[]{:S(2)}) collective-permute-start(bf16[256,512]{1,0:T(8,128)(2,1)S(1)} %get-tuple-element.59), channel_id=1, source_target_pairs={{0,120},{8,0},{16,8},{24,16},{32,24},{40,32},{48,40},{56,48},{64,5... | collective-permute-start | bytes 786440 | tf_op jit(solution)/shard_map/ppermute | solution.py:29
  148.7 3.6 %collective-permute-start.17 = (bf16[128,512]{1,0:T(8,128)(2,1)S(1)}, bf16[128,512]{1,0:T(8,128)(2,1)S(1)}, u32[]{:S(2)}, u32[]{:S(2)}) collective-permute-start(bf16[128,512]{1,0:T(8,128)(2,1)S(1)} %get-tuple-element.51.mine_ref), channel_id=1, source_target_pairs={{0,4},{2,6},{4,0},{6,2},{1,5},{3,7},{5,1},{7,3},{8,12},{10,14},{12... | collective-permute-start | bytes 393224 | tf_op jit(solution)/shard_map/ppermute | solution.py:33
  153.5 4.6 %collective-permute-done.10 = bf16[256,512]{1,0:T(8,128)(2,1)S(1)} collective-permute-done((bf16[256,512]{1,0:T(8,128)(2,1)S(1)}, bf16[256,512]{1,0:T(8,128)(2,1)S(1)}, u32[]{:S(2)}, u32[]{:S(2)}) %collective-permute-start.10) | collective-permute-done | bytes 262176 | tf_op jit(solution)/shard_map/ppermute | solution.py:29
  158.2 1.9 %collective-permute-start.12 = (bf16[1024,512]{1,0:T(8,128)(2,1)S(1)}, bf16[1024,512]{1,0:T(8,128)(2,1)S(1)}, u32[]{:S(2)}, u32[]{:S(2)}) collective-permute-start(bf16[1024,512]{1,0:T(8,128)(2,1)S(1)} %pad_maximum_fusion.1.early_ref), channel_id=1, source_target_pairs={{0,2},{2,0},{4,6},{6,4},{1,3},{3,1},{5,7},{7,5},{8,10},{10,8},{12,... | collective-permute-start | bytes 3145736 | tf_op jit(solution)/shard_map/ppermute | solution.py:33
  160.4 1.6 collective-permute-start.20
  162.0 7.1 %collective-permute-done.19 = bf16[128,512]{1,0:T(8,128)(2,1)S(1)} collective-permute-done((bf16[128,512]{1,0:T(8,128)(2,1)S(1)}, bf16[128,512]{1,0:T(8,128)(2,1)S(1)}, u32[]{:S(2)}, u32[]{:S(2)}) %collective-permute-start.19) | collective-permute-done | bytes 131104 | tf_op jit(solution)/shard_map/ppermute | solution.py:29
  169.2 4.2 %collective-permute-start.21 = (bf16[256,512]{1,0:T(8,128)(2,1)S(1)}, bf16[256,512]{1,0:T(8,128)(2,1)S(1)}, u32[]{:S(2)}, u32[]{:S(2)}) collective-permute-start(bf16[256,512]{1,0:T(8,128)(2,1)S(1)} %constant_dynamic-update-slice_fusion.1.late_ref), channel_id=1, source_target_pairs={{0,2},{2,0},{4,6},{6,4},{1,3},{3,1},{5,7},{7,5},{8,10},{10,8},{12,... | collective-permute-start | bytes 786440 | tf_op jit(solution)/shard_map/ppermute | solution.py:33
  174.6 6.4 %final.1 = f32[625,2,1024]{2,1,0:T(2,128)} custom-call(s32[1]{0:T(128)} %bitcast.at_ref, s32[1,1280]{1,0:T(1,128)S(1)} %broadcast_in_dim.37.ids_ref, bf16[1024,512]{1,0:T(8,128)(2,1)S(1)} %pad_maximum_fusion.1.early_ref, bf16[1024,512]{1,0:T(8,128)(2,1)S(1)} %collective-permute-done.12.early2_ref, ...), custom_call_target="tpu_custom_call" | custom-call | tf_op jit(solution)/shard_map/final/pallas_call | solution.py:253
  (118 shorter events, 16.6 us)
Async XLA Ops:
  7.0 16.5 %copy-start.9 = (s32[16,3]{0,1:T(4,128)S(1)}, s32[16,3]{0,1:T(4,128)}, u32[]{:S(2)}) copy-start(s32[16,3]{0,1:T(4,128)} %param.11) | copy-start | bytes 580
  15.1 78.3 %collective-permute-start.4 = (bf16[2,256,3072]{2,1,0:T(8,128)(2,1)}, bf16[2,256,3072]{2,1,0:T(8,128)(2,1)}, u32[]{:S(2)}, u32[]{:S(2)}) collective-permute-start(bf16[2,256,3072]{2,1,0:T(8,128)(2,1)} %get-tuple-element.39), channel_id=1, source_target_pairs={{0,8},{8,16},{16,24},{24,32},{32,40},{40,48},{48,56},{56,64},{64,7... | collective-permute-start | bytes 9437192 | tf_op jit(solution)/shard_map/ppermute | solution.py:29
  17.3 76.2 %collective-permute-start.5 = (bf16[2,256,3072]{2,1,0:T(8,128)(2,1)}, bf16[2,256,3072]{2,1,0:T(8,128)(2,1)}, u32[]{:S(2)}, u32[]{:S(2)}) collective-permute-start(bf16[2,256,3072]{2,1,0:T(8,128)(2,1)} %get-tuple-element.40), channel_id=1, source_target_pairs={{0,120},{8,0},{16,8},{24,16},{32,24},{40,32},{48,40},{56,48},{64,5... | collective-permute-start | bytes 9437192 | tf_op jit(solution)/shard_map/ppermute | solution.py:29
  37.5 17.6 %slice-start = ((s8[7766016]{0:T(1024)(128)(4,1)}), s8[4194304]{0:T(1024)(128)(4,1)S(1)}, s32[]{:S(2)}) async-start(s8[7766016]{0:T(1024)(128)(4,1)} %bitcast.40), calls=%async_computation | async-start | bytes 8388608
  88.3 38.6 %collective-permute-start.13 = (bf16[2,128,3072]{2,1,0:T(8,128)(2,1)}, bf16[2,128,3072]{2,1,0:T(8,128)(2,1)}, u32[]{:S(2)}, u32[]{:S(2)}) collective-permute-start(bf16[2,128,3072]{2,1,0:T(8,128)(2,1)} %get-tuple-element.47), channel_id=1, source_target_pairs={{0,8},{8,16},{16,24},{24,32},{32,40},{40,48},{48,56},{56,64},{64,7... | collective-permute-start | bytes 4718600 | tf_op jit(solution)/shard_map/ppermute | solution.py:29
  88.3 20.5 %copy-start.22 = (bf16[2,256,512]{2,1,0:T(8,128)(2,1)S(1)}, bf16[2,256,512]{2,1,0:T(8,128)(2,1)}, u32[]{:S(2)}) copy-start(bf16[2,256,512]{2,1,0:T(8,128)(2,1)} %get-tuple-element.36) | copy-start | bytes 1572868
  88.3 20.6 %copy-start.7 = (s32[1,1,256]{2,0,1:T(1,128)S(1)}, s32[1,1,256]{2,0,1:T(1,128)}, u32[]{:S(2)}) copy-start(s32[1,1,256]{2,0,1:T(1,128)} %get-tuple-element.63) | copy-start | bytes 3076
  88.3 20.6 %copy-start.8 = (s32[1,1,256]{2,0,1:T(1,128)S(1)}, s32[1,1,256]{2,0,1:T(1,128)}, u32[]{:S(2)}) copy-start(s32[1,1,256]{2,0,1:T(1,128)} %get-tuple-element.74) | copy-start | bytes 3076
  88.4 20.6 %copy-start.12 = (pred[256]{0:T(512)(128)(4,1)S(1)}, pred[256]{0:T(512)(128)(4,1)}, u32[]{:S(2)}) copy-start(pred[256]{0:T(512)(128)(4,1)} %get-tuple-element.54) | copy-start | bytes 772
  88.4 20.6 %copy-start.13 = (pred[256]{0:T(512)(128)(4,1)S(1)}, pred[256]{0:T(512)(128)(4,1)}, u32[]{:S(2)}) copy-start(pred[256]{0:T(512)(128)(4,1)} %get-tuple-element.55) | copy-start | bytes 772
  88.4 21.8 %copy-start.10 = (pred[256]{0:T(512)(128)(4,1)S(1)}, pred[256]{0:T(512)(128)(4,1)}, u32[]{:S(2)}) copy-start(pred[256]{0:T(512)(128)(4,1)} %get-tuple-element.53) | copy-start | bytes 772
  88.4 21.8 %copy-start.11 = (pred[256]{0:T(512)(128)(4,1)S(1)}, pred[256]{0:T(512)(128)(4,1)}, u32[]{:S(2)}) copy-start(pred[256]{0:T(512)(128)(4,1)} %get-tuple-element.57) | copy-start | bytes 772
  88.4 41.0 %collective-permute-start.14 = (bf16[2,128,3072]{2,1,0:T(8,128)(2,1)}, bf16[2,128,3072]{2,1,0:T(8,128)(2,1)}, u32[]{:S(2)}, u32[]{:S(2)}) collective-permute-start(bf16[2,128,3072]{2,1,0:T(8,128)(2,1)} %get-tuple-element.48), channel_id=1, source_target_pairs={{0,120},{8,0},{16,8},{24,16},{32,24},{40,32},{48,40},{56,48},{64,5... | collective-permute-start | bytes 4718600 | tf_op jit(solution)/shard_map/ppermute | solution.py:29
  93.4 24.1 %copy-start.5 = (f32[2,256,512]{2,1,0:T(8,128)S(1)}, f32[2,256,512]{2,1,0:T(8,128)}, u32[]{:S(2)}) copy-start(f32[2,256,512]{2,1,0:T(8,128)} %get-tuple-element.35.keep_ref) | copy-start | bytes 3145732
  107.4 4.7 %collective-permute-start.6 = (bf16[2,384,512]{2,1,0:T(8,128)(2,1)}, bf16[2,384,512]{2,1,0:T(8,128)(2,1)S(1)}, u32[]{:S(2)}, u32[]{:S(2)}) collective-permute-start(bf16[2,384,512]{2,1,0:T(8,128)(2,1)} %get-tuple-element.42), channel_id=1, source_target_pairs={{0,2},{2,0},{4,6},{6,4},{1,3},{3,1},{5,7},{7,5},{8,10},{10,8},{12,... | collective-permute-start | bytes 2359304 | tf_op jit(solution)/shard_map/ppermute | solution.py:33
  108.9 7.3 %collective-permute-start = (bf16[2,256,512]{2,1,0:T(8,128)(2,1)S(1)}, bf16[2,256,512]{2,1,0:T(8,128)(2,1)S(1)}, u32[]{:S(2)}, u32[]{:S(2)}) collective-permute-start(bf16[2,256,512]{2,1,0:T(8,128)(2,1)S(1)} %copy-done.22), channel_id=1, source_target_pairs={{0,2},{2,0},{4,6},{6,4},{1,3},{3,1},{5,7},{7,5},{8,10},{10,8},{12,... | collective-permute-start | bytes 1572872 | tf_op jit(solution)/shard_map/ppermute | solution.py:33
  113.6 26.3 %collective-permute-start.9 = (bf16[384,512]{1,0:T(8,128)(2,1)S(1)}, bf16[384,512]{1,0:T(8,128)(2,1)S(1)}, u32[]{:S(2)}, u32[]{:S(2)}) collective-permute-start(bf16[384,512]{1,0:T(8,128)(2,1)S(1)} %get-tuple-element.44), channel_id=1, source_target_pairs={{0,5},{1,4},{2,7},{3,6},{4,1},{5,0},{6,3},{7,2},{8,13},{9,12},{10,... | collective-permute-start | bytes 1179656 | tf_op jit(solution)/shard_map/ppermute | solution.py:224
  116.2 26.5 %collective-permute-start.7 = (bf16[384,512]{1,0:T(8,128)(2,1)S(1)}, bf16[384,512]{1,0:T(8,128)(2,1)S(1)}, u32[]{:S(2)}, u32[]{:S(2)}) collective-permute-start(bf16[384,512]{1,0:T(8,128)(2,1)S(1)} %get-tuple-element.44), channel_id=1, source_target_pairs={{0,1},{1,0},{2,3},{3,2},{4,5},{5,4},{6,7},{7,6},{8,9},{9,8},{10,11... | collective-permute-start | bytes 1179656 | tf_op jit(solution)/shard_map/ppermute | solution.py:33
  116.2 22.4 %collective-permute-start.8 = (bf16[384,512]{1,0:T(8,128)(2,1)S(1)}, bf16[384,512]{1,0:T(8,128)(2,1)S(1)}, u32[]{:S(2)}, u32[]{:S(2)}) collective-permute-start(bf16[384,512]{1,0:T(8,128)(2,1)S(1)} %get-tuple-element.43.mine_ref), channel_id=1, source_target_pairs={{0,4},{2,6},{4,0},{6,2},{1,5},{3,7},{5,1},{7,3},{8,12},{10,14},{12... | collective-permute-start | bytes 1179656 | tf_op jit(solution)/shard_map/ppermute | solution.py:33
  126.9 21.0 %collective-permute-start.3 = (bf16[256,512]{1,0:T(8,128)(2,1)S(1)}, bf16[256,512]{1,0:T(8,128)(2,1)S(1)}, u32[]{:S(2)}, u32[]{:S(2)}) collective-permute-start(bf16[256,512]{1,0:T(8,128)(2,1)S(1)} %get-tuple-element.38), channel_id=1, source_target_pairs={{0,5},{1,4},{2,7},{3,6},{4,1},{5,0},{6,3},{7,2},{8,13},{9,12},{10,... | collective-permute-start | bytes 786440 | tf_op jit(solution)/shard_map/ppermute | solution.py:224
  129.4 18.6 %collective-permute-start.1 = (bf16[256,512]{1,0:T(8,128)(2,1)S(1)}, bf16[256,512]{1,0:T(8,128)(2,1)S(1)}, u32[]{:S(2)}, u32[]{:S(2)}) collective-permute-start(bf16[256,512]{1,0:T(8,128)(2,1)S(1)} %get-tuple-element.38), channel_id=1, source_target_pairs={{0,1},{1,0},{2,3},{3,2},{4,5},{5,4},{6,7},{7,6},{8,9},{9,8},{10,11... | collective-permute-start | bytes 786440 | tf_op jit(solution)/shard_map/ppermute | solution.py:33
  138.5 9.3 %collective-permute-start.2 = (bf16[256,512]{1,0:T(8,128)(2,1)S(1)}, bf16[256,512]{1,0:T(8,128)(2,1)S(1)}, u32[]{:S(2)}, u32[]{:S(2)}) collective-permute-start(bf16[256,512]{1,0:T(8,128)(2,1)S(1)} %get-tuple-element.37.mine_ref), channel_id=1, source_target_pairs={{0,4},{2,6},{4,0},{6,2},{1,5},{3,7},{5,1},{7,3},{8,12},{10,14},{12... | collective-permute-start | bytes 786440 | tf_op jit(solution)/shard_map/ppermute | solution.py:33
  139.9 8.4 %collective-permute-start.15 = (bf16[2,128,512]{2,1,0:T(8,128)(2,1)}, bf16[2,128,512]{2,1,0:T(8,128)(2,1)S(1)}, u32[]{:S(2)}, u32[]{:S(2)}) collective-permute-start(bf16[2,128,512]{2,1,0:T(8,128)(2,1)} %get-tuple-element.50), channel_id=1, source_target_pairs={{0,2},{2,0},{4,6},{6,4},{1,3},{3,1},{5,7},{7,5},{8,10},{10,8},{12,... | collective-permute-start | bytes 786440 | tf_op jit(solution)/shard_map/ppermute | solution.py:33
  143.1 10.4 %collective-permute-start.11 = (bf16[256,512]{1,0:T(8,128)(2,1)S(1)}, bf16[256,512]{1,0:T(8,128)(2,1)S(1)}, u32[]{:S(2)}, u32[]{:S(2)}) collective-permute-start(bf16[256,512]{1,0:T(8,128)(2,1)S(1)} %get-tuple-element.59), channel_id=1, source_target_pairs={{0,120},{8,0},{16,8},{24,16},{32,24},{40,32},{48,40},{56,48},{64,5... | collective-permute-start | bytes 786440 | tf_op jit(solution)/shard_map/ppermute | solution.py:29
  147.8 10.3 %collective-permute-start.10 = (bf16[256,512]{1,0:T(8,128)(2,1)S(1)}, bf16[256,512]{1,0:T(8,128)(2,1)S(1)}, u32[]{:S(2)}, u32[]{:S(2)}) collective-permute-start(bf16[256,512]{1,0:T(8,128)(2,1)S(1)} %pad_maximum_fusion.2), channel_id=1, source_target_pairs={{0,8},{8,16},{16,24},{24,32},{32,40},{40,48},{48,56},{56,64},{64,7... | collective-permute-start | bytes 786440 | tf_op jit(solution)/shard_map/ppermute | solution.py:29
  148.4 11.7 %collective-permute-start.18 = (bf16[128,512]{1,0:T(8,128)(2,1)S(1)}, bf16[128,512]{1,0:T(8,128)(2,1)S(1)}, u32[]{:S(2)}, u32[]{:S(2)}) collective-permute-start(bf16[128,512]{1,0:T(8,128)(2,1)S(1)} %get-tuple-element.52), channel_id=1, source_target_pairs={{0,5},{1,4},{2,7},{3,6},{4,1},{5,0},{6,3},{7,2},{8,13},{9,12},{10,... | collective-permute-start | bytes 393224 | tf_op jit(solution)/shard_map/ppermute | solution.py:224
  148.7 11.4 %collective-permute-start.16 = (bf16[128,512]{1,0:T(8,128)(2,1)S(1)}, bf16[128,512]{1,0:T(8,128)(2,1)S(1)}, u32[]{:S(2)}, u32[]{:S(2)}) collective-permute-start(bf16[128,512]{1,0:T(8,128)(2,1)S(1)} %get-tuple-element.52), channel_id=1, source_target_pairs={{0,1},{1,0},{2,3},{3,2},{4,5},{5,4},{6,7},{7,6},{8,9},{9,8},{10,11... | collective-permute-start | bytes 393224 | tf_op jit(solution)/shard_map/ppermute | solution.py:33
  148.7 11.4 %collective-permute-start.17 = (bf16[128,512]{1,0:T(8,128)(2,1)S(1)}, bf16[128,512]{1,0:T(8,128)(2,1)S(1)}, u32[]{:S(2)}, u32[]{:S(2)}) collective-permute-start(bf16[128,512]{1,0:T(8,128)(2,1)S(1)} %get-tuple-element.51.mine_ref), channel_id=1, source_target_pairs={{0,4},{2,6},{4,0},{6,2},{1,5},{3,7},{5,1},{7,3},{8,12},{10,14},{12... | collective-permute-start | bytes 393224 | tf_op jit(solution)/shard_map/ppermute | solution.py:33
  158.2 16.4 %collective-permute-start.12 = (bf16[1024,512]{1,0:T(8,128)(2,1)S(1)}, bf16[1024,512]{1,0:T(8,128)(2,1)S(1)}, u32[]{:S(2)}, u32[]{:S(2)}) collective-permute-start(bf16[1024,512]{1,0:T(8,128)(2,1)S(1)} %pad_maximum_fusion.1.early_ref), channel_id=1, source_target_pairs={{0,2},{2,0},{4,6},{6,4},{1,3},{3,1},{5,7},{7,5},{8,10},{10,8},{12,... | collective-permute-start | bytes 3145736 | tf_op jit(solution)/shard_map/ppermute | solution.py:33
  160.4 8.8 %collective-permute-start.20 = (bf16[128,512]{1,0:T(8,128)(2,1)S(1)}, bf16[128,512]{1,0:T(8,128)(2,1)S(1)}, u32[]{:S(2)}, u32[]{:S(2)}) collective-permute-start(bf16[128,512]{1,0:T(8,128)(2,1)S(1)} %sum4.5), channel_id=1, source_target_pairs={{0,120},{8,0},{16,8},{24,16},{32,24},{40,32},{48,40},{56,48},{64,5... | collective-permute-start | bytes 393224 | tf_op jit(solution)/shard_map/ppermute | solution.py:29
  162.0 7.1 %collective-permute-start.19 = (bf16[128,512]{1,0:T(8,128)(2,1)S(1)}, bf16[128,512]{1,0:T(8,128)(2,1)S(1)}, u32[]{:S(2)}, u32[]{:S(2)}) collective-permute-start(bf16[128,512]{1,0:T(8,128)(2,1)S(1)} %sum4.5), channel_id=1, source_target_pairs={{0,8},{8,16},{16,24},{24,32},{32,40},{40,48},{48,56},{56,64},{64,7... | collective-permute-start | bytes 393224 | tf_op jit(solution)/shard_map/ppermute | solution.py:29
  169.2 5.3 %collective-permute-start.21 = (bf16[256,512]{1,0:T(8,128)(2,1)S(1)}, bf16[256,512]{1,0:T(8,128)(2,1)S(1)}, u32[]{:S(2)}, u32[]{:S(2)}) collective-permute-start(bf16[256,512]{1,0:T(8,128)(2,1)S(1)} %constant_dynamic-update-slice_fusion.1.late_ref), channel_id=1, source_target_pairs={{0,2},{2,0},{4,6},{6,4},{1,3},{3,1},{5,7},{7,5},{8,10},{10,8},{12,... | collective-permute-start | bytes 786440 | tf_op jit(solution)/shard_map/ppermute | solution.py:33
  (15 other events, 109.1 us)

commit v2 on v1

--- a/solution.py
+++ b/solution.py
@@ -16,6 +16,7 @@
 TILE = 512
 PICK_MB = 20
 CORR_MB = 56
+SPLIT = 128
 F32 = jnp.float32
 BF16 = jnp.bfloat16
 
@@ -62,7 +63,7 @@
             row += count
 
 
-def pick(groups, rows):
+def pick(groups, rows, megabytes=PICK_MB):
     counts = [sum(index.shape[0] for index in group) for group in groups]
     index = jnp.concatenate([index for group in groups for index in group])
     (total,), (_, chans, freqs) = index.shape, rows.shape
@@ -76,54 +77,58 @@
         ],
         out_specs=[pl.BlockSpec((2, count, TILE), lambda i: (0, 0, i)) for count in counts],
         scratch_shapes=[pltpu.VMEM((total, chans), BF16)],
-        compiler_params=params(PICK_MB),
+        compiler_params=params(megabytes),
         cost_estimate=cost(4 * total * chans * freqs, 4 * (chans + total) * freqs),
         name="pick",
     )(index[:, None], rows)
 
 
-def table_kernel(coarse_ref, fine_ref, sign_ref, out_ref):
-    cos_b, sin_b = fine_ref[0], fine_ref[1]
+def table_kernel(cos_a_ref, sin_a_ref, cos_b_ref, sin_b_ref, sign_ref, cos_ref, sin_ref):
+    cos_b, sin_b = cos_b_ref[...], sin_b_ref[...]
     width = cos_b.shape[1]
     for step in range(2 * QUARTER // width):
-        cos_a, sin_a = coarse_ref[0, :, step : step + 1], coarse_ref[1, :, step : step + 1]
+        cos_a, sin_a = cos_a_ref[:, step : step + 1], sin_a_ref[:, step : step + 1]
         cols = slice(step * width, (step + 1) * width)
-        out_ref[0, :, cols] = (cos_a * cos_b - sin_a * sin_b).astype(BF16)
-        out_ref[1, :, cols] = (sign_ref[0] * (sin_a * cos_b + cos_a * sin_b)).astype(BF16)
-
-
-def lag_table(freq_index, core, sign):
-    freqs, width = freq_index.shape[0], 128
+        cos_ref[:, cols] = (cos_a * cos_b - sin_a * sin_b).astype(BF16)
+        sin_ref[:, cols] = (sign_ref[0] * (sin_a * cos_b + cos_a * sin_b)).astype(BF16)
+
+
+def waves(doubled, freq):
+    angle = jnp.mod(doubled * freq, 4 * FREQ).astype(F32) * (math.pi / (2 * FREQ))
+    return jnp.cos(angle), jnp.sin(angle)
+
+
+def lag_waves(freq_index, core):
+    width = 128
     steps = 2 * QUARTER // width
-    step = jnp.arange(steps, dtype=jnp.int32)
+    flat = jnp.arange(freq_index.shape[0] * steps, dtype=jnp.int32)
+    step = flat % steps
     start = (core ^ (step // (steps // 2))) * QUARTER + (step % (steps // 2)) * width
-
-    def waves(doubled, freq):
-        angle = jnp.mod(doubled * freq, 4 * FREQ).astype(F32) * (math.pi / (2 * FREQ))
-        return jnp.stack([jnp.cos(angle), jnp.sin(angle)])
-
-    coarse = waves(2 * start[:, None], freq_index[None, :]).transpose(0, 2, 1)
+    coarse = lax.optimization_barrier(waves(2 * start, freq_index[0] + flat // steps))
+    cos_a, sin_a = [value.reshape(-1, steps) for value in coarse]
     odd = 2 * jnp.arange(width, dtype=jnp.int32) + 1
-    fine = waves(odd[None, :], freq_index[:, None])
+    cos_a, sin_a = lax.optimization_barrier((cos_a, sin_a))
+    return (cos_a, sin_a) + waves(odd[None, :], freq_index[:, None])
+
+
+def lag_table(four, sign):
+    freqs = four[0].shape[0]
     return pl.pallas_call(
         table_kernel,
-        out_shape=jax.ShapeDtypeStruct((2, freqs, 2 * QUARTER), BF16),
+        out_shape=[jax.ShapeDtypeStruct((freqs, 2 * QUARTER), BF16)] * 2,
         grid=(freqs // TILE,),
-        in_specs=[
-            pl.BlockSpec((2, TILE, steps), lambda i: (0, i, 0)),
-            pl.BlockSpec((2, TILE, width), lambda i: (0, i, 0)),
-            pl.BlockSpec(memory_space=pltpu.SMEM),
-        ],
-        out_specs=pl.BlockSpec((2, TILE, 2 * QUARTER), lambda i: (0, i, 0)),
-        compiler_params=params(),
+        in_specs=[pl.BlockSpec((TILE, v.shape[1]), lambda i: (i, 0)) for v in four]
+        + [pl.BlockSpec(memory_space=pltpu.SMEM)],
+        out_specs=[pl.BlockSpec((TILE, 2 * QUARTER), lambda i: (i, 0))] * 2,
+        compiler_params=params(CORR_MB),
         cost_estimate=cost(12 * freqs * LAGS, 4 * freqs * LAGS),
         name="table",
-    )(coarse, fine, sign[None])
+    )(*four, sign[None])
 
 
 def corr_kernel(count, *refs):
     firsts, seconds = refs[:count], refs[count : 2 * count]
-    turn_ref, table_ref, keep_ref, send_ref, cos_acc, sin_acc = refs[2 * count :]
+    turn_ref, cos_ref, sin_ref, keep_ref, send_ref, cos_acc, sin_acc = refs[2 * count :]
     step = pl.program_id(0)
 
     @pl.when(step == 0)
@@ -141,8 +146,8 @@
         turned_re = (real * turn_cos + imag * turn_sin).astype(BF16)
         turned_im = (imag * turn_cos - real * turn_sin).astype(BF16)
         here = slice(row, row + first_ref.shape[1])
-        cos_acc[here] += dot(turned_re, table_ref[0])
-        sin_acc[here] += dot(turned_im, table_ref[1])
+        cos_acc[here] += dot(turned_re, cos_ref[...])
+        sin_acc[here] += dot(turned_im, sin_ref[...])
         row += first_ref.shape[1]
 
     @pl.when(step == pl.num_programs(0) - 1)
@@ -159,7 +164,7 @@
 def correlate(pairs, turn, table):
     firsts, seconds = zip(*pairs)
     rows = sum(count for _, count, _ in firsts)
-    freqs = table.shape[1]
+    freqs = table[0].shape[0]
 
     def spec(value):
         _, count, place = value
@@ -176,7 +181,8 @@
         in_specs=[spec(value) for value in flat]
         + [
             pl.BlockSpec((2, TILE), lambda i: (0, i)),
-            pl.BlockSpec((2, TILE, 2 * QUARTER), lambda i: (0, i, 0)),
+            pl.BlockSpec((TILE, 2 * QUARTER), lambda i: (i, 0)),
+            pl.BlockSpec((TILE, 2 * QUARTER), lambda i: (i, 0)),
         ],
         out_specs=(
             pl.BlockSpec((2, rows, QUARTER), lambda i: (0, 0, 0)),
@@ -186,7 +192,7 @@
         compiler_params=params(CORR_MB),
         cost_estimate=cost(4 * rows * freqs * LAGS, 4 * freqs * LAGS + 16 * rows * freqs),
         name="corr",
-    )(*[value[0] for value in flat], turn, table)
+    )(*[value[0] for value in flat], turn, *table)
 
 
 def fold_kernel(keep_ref, other_ref, mine_ref, far_ref):
@@ -201,11 +207,16 @@
     )(keep, other)
 
 
-def sum_kernel(flip_ref, mine_ref, near_ref, far_ref, across_ref, out_ref):
-    total = (mine_ref[...].astype(F32) + near_ref[...].astype(F32)) + (
-        far_ref[...].astype(F32) + across_ref[...].astype(F32)
-    )
-    total = total.astype(BF16)
+def add_kernel(mine_ref, near_ref, out_ref):
+    out_ref[...] = (mine_ref[...].astype(F32) + near_ref[...].astype(F32)).astype(BF16)
+
+
+def sum_kernel(flip_ref, *refs):
+    parts, out_ref = refs[:-1], refs[-1]
+    sums = [
+        a[...].astype(F32) + b[...].astype(F32) for a, b in zip(parts[::2], parts[1::2])
+    ]
+    total = functools.reduce(lambda a, b: a + b, sums).astype(BF16)
     size = total.shape[1]
     row = lax.broadcasted_iota(jnp.int32, (size, size), 0)
     col = lax.broadcasted_iota(jnp.int32, (size, size), 1)
@@ -214,22 +225,42 @@
     out_ref[...] = dot(total, order).astype(BF16)
 
 
-def reduced(partial, flip):
+def summed(flip, parts):
+    vmem = pl.BlockSpec(memory_space=pltpu.VMEM)
+    return pl.pallas_call(
+        sum_kernel,
+        out_shape=jax.ShapeDtypeStruct(parts[0].shape, BF16),
+        in_specs=[pl.BlockSpec(memory_space=pltpu.SMEM)] + [vmem] * len(parts),
+        compiler_params=params(),
+        name="sum",
+    )(flip[None], *parts)
+
+
+def folded(partial):
     keep, send = partial
-    mine, far = fold(keep, swapped(send, "seg", 1))
+    return fold(keep, swapped(send, "seg", 1))
+
+
+def near_sum(mine, far):
+    return pl.pallas_call(
+        add_kernel,
+        out_shape=jax.ShapeDtypeStruct(mine.shape, BF16),
+        compiler_params=params(),
+        name="add",
+    )(mine, swapped(far, "lag", 1))
+
+
+def far_sum(both, flip):
+    return summed(flip, [both, swapped(both, "seg", 2)])
+
+
+def direct_sum(mine, far, flip):
     near = swapped(far, "lag", 1)
     opposite = swapped(mine, "seg", 2)
     seg, lag = lax.axis_size("seg"), lax.axis_size("lag")
     pairs = [(s * lag + g, (s ^ 2) * lag + (g ^ 1)) for s in range(seg) for g in range(lag)]
     across = lax.ppermute(far, ("seg", "lag"), pairs)
-    vmem = pl.BlockSpec(memory_space=pltpu.VMEM)
-    return pl.pallas_call(
-        sum_kernel,
-        out_shape=jax.ShapeDtypeStruct(mine.shape, BF16),
-        in_specs=[pl.BlockSpec(memory_space=pltpu.SMEM)] + [vmem] * 4,
-        compiler_params=params(),
-        name="sum4",
-    )(flip[None], mine, near, opposite, across)
+    return summed(flip, [mine, near, opposite, across])
 
 
 def final_kernel(at_ref, ids_ref, early_ref, early2_ref, late_ref, late2_ref, out_ref):
@@ -272,52 +303,54 @@
     rows = own.transpose(1, 0, 2)
     before, before2 = (block - 1) % blocks, (block - 2) % blocks
 
-    first_up = [pair_local[block, 1, HALF:], pair_local[block, 2, :HALF]]
-    first_down = [pair_partner[before, 1, :HALF], pair_partner[before2, 2, :HALF]]
-    last_up, last_down = pair_local[block, 2, HALF:], pair_partner[before2, 2, HALF:]
+    first_up = [pair_local[block, 1, HALF:], pair_local[block, 2, :SPLIT]]
+    first_down = [pair_partner[before, 1, :HALF], pair_partner[before2, 2, :SPLIT]]
+    last_up, last_down = pair_local[block, 2, SPLIT:], pair_partner[before2, 2, SPLIT:]
     picked = pick([first_up, first_down], rows)
     picked, rows, zero = lax.optimization_barrier((picked, rows, jnp.int32(0)))
     from_before, from_after = [shifted(picked[0], 1)], [shifted(picked[1], -1)]
 
     freq_index = lag_index * half_freq + jnp.arange(half_freq, dtype=jnp.int32) + 1 + zero
+    four = lag_waves(freq_index, core)
+    four, last_up, last_down = lax.optimization_barrier((four, last_up, last_down))
+    local = [
+        pair_local[block, 0],
+        pair_partner[block, 0],
+        pair_local[block, 1, :HALF],
+        pair_partner[before, 1, HALF:],
+    ]
+    up, down, local = pick([[last_up], [last_down], local], rows, CORR_MB)
+    up, down, local, four = lax.optimization_barrier((up, down, local, four))
+    from_before.append(shifted(up, 1))
+    from_after.append(shifted(down, -1))
     sign = jnp.where(lag_index == 0, 1.0, -1.0).astype(F32)
-    table = lag_table(freq_index, core, sign)
+    table = lag_table(four, sign)
     angle = freq_index.astype(F32) * (math.pi / (2 * FREQ))
     turn = jnp.stack([jnp.cos(angle), jnp.sin(angle)])
 
-    (local,) = pick(
-        [
-            [
-                pair_local[block, 0] + zero,
-                pair_partner[block, 0],
-                pair_local[block, 1, :HALF],
-                pair_partner[before, 1, HALF:],
-            ]
-        ],
-        rows,
-    )
     flip = 1 - lag_index
 
     def at(value, count, place):
         return value, count, place
 
-    def total(pairs):
-        return reduced(correlate(pairs, turn, table), flip)
-
-    partial0 = correlate([(at(local, slots, 0), at(local, slots, 1))], turn, table)
-    partial0, last_up, last_down = lax.optimization_barrier((partial0, last_up, last_down))
-    picked = pick([[last_up], [last_down]], rows)
-    from_before.append(shifted(picked[0], 1))
-    from_after.append(shifted(picked[1], -1))
-    corr0 = reduced(partial0, flip)
-    corr1 = total(
-        [
-            (at(local, HALF, 4), at(from_after[0], HALF, 0)),
-            (at(from_before[0], HALF, 0), at(local, HALF, 5)),
-            (at(from_before[0], HALF, 1), at(from_after[0], HALF, 1)),
-        ]
+    half0 = folded(correlate([(at(local, slots, 0), at(local, slots, 1))], turn, table))
+    both0, above, below = lax.optimization_barrier(
+        (near_sum(*half0), from_before[0], from_after[0])
     )
-    corr2 = total([(at(from_before[1], HALF, 0), at(from_after[1], HALF, 0))])
+    pairs = [
+        (at(local, HALF, 4), at(below, HALF, 0)),
+        (at(above, HALF, 0), at(local, HALF, 5)),
+        (at(above, SPLIT, HALF // SPLIT), at(below, SPLIT, HALF // SPLIT)),
+    ]
+    half1 = folded(correlate(pairs, turn, table))
+    corr0 = far_sum(both0, flip)
+    both1, above, below = lax.optimization_barrier(
+        (near_sum(*half1), from_before[1], from_after[1])
+    )
+    corr1 = far_sum(both1, flip)
+    tail = slots - SPLIT
+    half2 = folded(correlate([(at(above, tail, 0), at(below, tail, 0))], turn, table))
+    corr2 = direct_sum(*half2, flip)
     to_after = jnp.concatenate([corr1[:HALF], corr1[2 * HALF :]])
     to_before = corr1[HALF:]
     early = jnp.concatenate(
@@ -345,11 +378,11 @@
             near0[:HALF],
             near1[HALF:],
             near1[:HALF],
-            far1[:HALF],
+            far1[:SPLIT],
             near0[HALF:],
-            far0[:HALF],
-            far1[HALF:],
-            far0[HALF:],
+            far0[:SPLIT],
+            far1[SPLIT:],
+            far0[SPLIT:],
         ]
     )[None, :]
     place = core ^ flip

time: 181 us -> 173 us (0.956)
  local copies, waits for them, and re-layouts: 22.8 us -> 17.6 us
  other arithmetic: 19.3 us -> 15.2 us
    ppermute x8, waiting for transfers between devices: 22.2 us -> 6.59 us  [shifted(): lax.ppermute(value, 'chan', route('chan', lambda i: (i + distance) % count))]
    ppermute x11, waiting for transfers between devices: 1.16 us -> 15.7 us  [swapped(): return lax.ppermute(value, axis, route(axis, lambda i: i ^ bit))]
    unnamed x59 -> x29, local copies, waits for them, and re-layouts: 18.4 us -> 8.9 us
    sin x0 -> x2, other arithmetic: none -> 9.27 us  [waves(): return (jnp.cos(angle), jnp.sin(angle))]
    cos x3 -> x0, other arithmetic: 8.94 us -> none  [the longest x2 8.6 us: waves(): return jnp.stack([jnp.cos(angle), jnp.sin(angle)])]
    reshape x0 -> x2, local copies, waits for them, and re-layouts: none -> 4.02 us  [lag_waves(): cos_a, sin_a = [value.reshape(-1, steps) for value in coarse]]
    ppermute x3 -> x1, starting transfers between devices: 5.31 us -> 1.82 us  [direct_sum(): across = lax.ppermute(far, ('seg', 'lag'), pairs)]
    ppermute x8, starting transfers between devices: 18.4 us -> 21.7 us  [shifted(): lax.ppermute(value, 'chan', route('chan', lambda i: (i + distance) % count))]
  transfers between devices with their start and end apart: 22 -> 20, of which waited for: 5 -> 9; matrix products, arithmetic and copies ran while one was open for 12% -> 13% of each run, Pallas kernels for 33% -> 36%
where the time goes in v2:
time: 173 us; the launch traced here: 172 us
  Pallas kernels  75.6 us (44%)
  starting transfers between devices  40.8 us (24%)
  waiting for transfers between devices  22.3 us (13%)
  local copies, waits for them, and re-layouts  17.6 us (10%)
  other arithmetic  15.2 us (9%)
    pallas_call x3, Pallas kernels, correlate(): pl.pallas_call(functools.partial(corr_kernel, len(pairs)), out_shape=(jax...  33.8 us
    pallas_call x2, Pallas kernels, pick(): pl.pallas_call(pick_kernel, out_shape=[jax.ShapeDtypeStruct((2, count, fr...  22 us
    ppermute x8, starting transfers between devices, shifted(): lax.ppermute(value, 'chan', route('chan', lambda i: (i + distance) % count))  21.7 us
    ppermute x11, starting transfers between devices, swapped(): return lax.ppermute(value, axis, route(axis, lambda i: i ^ bit))  17.3 us
    ppermute x11, waiting for transfers between devices, swapped(): return lax.ppermute(value, axis, route(axis, lambda i: i ^ bit))  15.7 us
    pallas_call x1, Pallas kernels, lag_table(): pl.pallas_call(table_kernel, out_shape=[jax.ShapeDtypeStruct((freqs, 2 *...  12.1 us
    sin x2, other arithmetic, waves(): return (jnp.cos(angle), jnp.sin(angle))  9.27 us
    unnamed x29, local copies, waits for them, and re-layouts  8.9 us
  transfers between devices with their start and end apart: 20, of which 9 were waited for; matrix products, arithmetic and copies ran while one was open for 13% of the time, Pallas kernels for 36%

profile of v2, /device:TPU:1, one launch (start us, length us, event | category | flops | bytes accessed | tf_op | source)
XLA Modules:
  0.0 171.8 jit_solution(13751467652189088582)
XLA Ops:
  1.6 5.5 %copy.12 = bf16[1,625,2,3072]{3,1,2,0:T(8,128)(2,1)S(1)} copy(bf16[1,625,2,3072]{3,2,1,0:T(2,128)(2,1)} %param.6) | data formatting | bytes 15360000 | tf_op args[0]
  7.1 8.0 %pick.2 = (bf16[2,256,3072]{2,1,0:T(8,128)(2,1)}, bf16[2,256,3072]{2,1,0:T(8,128)(2,1)}) custom-call(s32[512,1]{1,0:T(8,128)S(1)} %copy.9.index_ref, bf16[2,625,3072]{2,1,0:T(8,128)(2,1)S(1)} %bitcast.43), custom_call_target="tpu_custom_call" | custom-call | flops 3932160000 | bytes 13971456 | tf_op jit(solution)/shard_map/pick/pallas_call | solution.py:70
  15.1 2.1 %collective-permute-start.2 = (bf16[2,256,3072]{2,1,0:T(8,128)(2,1)}, bf16[2,256,3072]{2,1,0:T(8,128)(2,1)}, u32[]{:S(2)}, u32[]{:S(2)}) collective-permute-start(bf16[2,256,3072]{2,1,0:T(8,128)(2,1)} %get-tuple-element.79), channel_id=1, source_target_pairs={{0,8},{8,16},{16,24},{24,32},{32,40},{40,48},{48,56},{56,64},{64,7... | collective-permute-start | bytes 9437192 | tf_op jit(solution)/shard_map/ppermute | solution.py:30
  17.3 4.9 %collective-permute-start.3 = (bf16[2,256,3072]{2,1,0:T(8,128)(2,1)}, bf16[2,256,3072]{2,1,0:T(8,128)(2,1)}, u32[]{:S(2)}, u32[]{:S(2)}) collective-permute-start(bf16[2,256,3072]{2,1,0:T(8,128)(2,1)} %get-tuple-element.80), channel_id=1, source_target_pairs={{0,120},{8,0},{16,8},{24,16},{32,24},{40,32},{48,40},{56,48},{64,5... | collective-permute-start | bytes 9437192 | tf_op jit(solution)/shard_map/ppermute | solution.py:30
  24.0 2.0 %reshape.65.cos_a_ref = f32[3072,8]{1,0:T(8,128)} reshape(f32[24576]{0:T(1024)S(1)} %get-tuple-element.54) | data formatting | bytes 196608 | tf_op jit(solution)/shard_map/reshape | solution.py:108
  26.0 2.0 %reshape.66.sin_a_ref = f32[3072,8]{1,0:T(8,128)} reshape(f32[24576]{0:T(1024)S(1)} %get-tuple-element.55) | data formatting | bytes 196608 | tf_op jit(solution)/shard_map/reshape | solution.py:108
  28.0 8.1 %fusion.4 = (f32[3072,128]{1,0:T(8,128)}, f32[3072,128]{1,0:T(8,128)}) fusion(s32[3072]{0:T(1024)S(1)} %add_add_fusion, s32[128]{0:T(128)S(1)} %multiply_add_fusion), kind=kLoop, calls=%fused_computation.7 | loop fusion | flops 3538944 | bytes 3158528 | tf_op jit(solution)/shard_map/sin | solution.py:98
  41.5 14.0 %pick.3 = (bf16[2,128,3072]{2,1,0:T(8,128)(2,1)}, bf16[2,128,3072]{2,1,0:T(8,128)(2,1)}, bf16[2,768,3072]{2,1,0:T(8,128)(2,1)}) custom-call(s32[1024,1]{1,0:T(8,128)} %copy.10.index_ref, bf16[2,625,3072]{2,1,0:T(8,128)(2,1)} %bitcast.44), custom_call_target="tpu_custom_call" | custom-call | flops 7864320000 | bytes 20262912 | tf_op jit(solution)/shard_map/pick/pallas_call | solution.py:70
  55.5 12.1 %table.1 = (bf16[3072,1024]{1,0:T(8,128)(2,1)}, bf16[3072,1024]{1,0:T(8,128)(2,1)}) custom-call(f32[3072,8]{1,0:T(8,128)} %reshape.65.cos_a_ref, f32[3072,8]{1,0:T(8,128)} %reshape.66.sin_a_ref, f32[3072,128]{1,0:T(8,128)} %get-tuple-element.71.cos_b_ref, f32[3072,128]{1,0:T(8,128)} %get-tuple-element.72.sin_b_ref, f32[1]{0:T(128)} %bitcast.27.sign_ref), custom_call_target="tpu_custom_call" | custom-call | flops 75497472 | bytes 25165824 | tf_op jit(solution)/shard_map/table/pallas_call | solution.py:116
  68.6 11.2 %corr.3 = (f32[2,256,512]{2,1,0:T(8,128)}, bf16[2,256,512]{2,1,0:T(8,128)(2,1)}) custom-call(bf16[2,768,3072]{2,1,0:T(8,128)(2,1)} %get-tuple-element.68.refs_0_.refs_1_.refs_4_, bf16[2,768,3072]{2,1,0:T(8,128)(2,1)} %get-tuple-element.68.refs_0_.refs_1_.refs_4_, f32[2,3072]{1,0:T(2,128)} %pad_maximum_fusion.2.refs_2_.refs_6_, ...), custom_call_target="tpu_custom_call" | custom-call | flops 6442450944 | bytes 37748736 | tf_op jit(solution)/shard_map/corr/pallas_call | solution.py:174
  80.7 1.7 %collective-permute-done.other_ref = bf16[2,256,512]{2,1,0:T(8,128)(2,1)S(1)} collective-permute-done((bf16[2,256,512]{2,1,0:T(8,128)(2,1)}, bf16[2,256,512]{2,1,0:T(8,128)(2,1)S(1)}, u32[]{:S(2)}, u32[]{:S(2)}) %collective-permute-start) | collective-permute-done | bytes 524320 | tf_op jit(solution)/shard_map/ppermute | solution.py:34
  83.8 1.3 collective-permute-start.1
  85.1 4.8 %collective-permute-start.8 = (bf16[2,128,3072]{2,1,0:T(8,128)(2,1)S(1)}, bf16[2,128,3072]{2,1,0:T(8,128)(2,1)}, u32[]{:S(2)}, u32[]{:S(2)}) collective-permute-start(bf16[2,128,3072]{2,1,0:T(8,128)(2,1)S(1)} %copy-done.6), channel_id=1, source_target_pairs={{0,120},{8,0},{16,8},{24,16},{32,24},{40,32},{48,40},{56,48},{64,5... | collective-permute-start | bytes 4718600 | tf_op jit(solution)/shard_map/ppermute | solution.py:30
  89.8 1.6 collective-permute-done.1.near_ref
  91.6 13.7 %corr.4 = (f32[2,384,512]{2,1,0:T(8,128)}, bf16[2,384,512]{2,1,0:T(8,128)(2,1)}) custom-call(bf16[2,768,3072]{2,1,0:T(8,128)(2,1)} %get-tuple-element.68.refs_0_.refs_1_.refs_4_, bf16[2,256,3072]{2,1,0:T(8,128)(2,1)} %collective-permute-done.2.refs_1_.refs_2_, bf16[2,256,3072]{2,1,0:T(8,128)(2,1)} %collective-permute-done.2.refs_1_.refs_2_, ...), custom_call_target="tpu_custom_call" | custom-call | flops 9663676416 | bytes 44040192 | tf_op jit(solution)/shard_map/corr/pallas_call | solution.py:174
  106.3 1.4 and_select_fusion.2
  108.4 1.4 copy-done.1
  110.0 1.3 collective-permute-start.6
  112.5 8.0 %collective-permute-done.6.near_ref = bf16[384,512]{1,0:T(8,128)(2,1)S(1)} collective-permute-done((bf16[384,512]{1,0:T(8,128)(2,1)S(1)}, bf16[384,512]{1,0:T(8,128)(2,1)S(1)}, u32[]{:S(2)}, u32[]{:S(2)}) %collective-permute-start.6) | collective-permute-done | bytes 393248 | tf_op jit(solution)/shard_map/ppermute | solution.py:34
  120.6 3.1 %collective-permute-done.7.refs_0_ = bf16[2,128,3072]{2,1,0:T(8,128)(2,1)S(1)} collective-permute-done((bf16[2,128,3072]{2,1,0:T(8,128)(2,1)S(1)}, bf16[2,128,3072]{2,1,0:T(8,128)(2,1)S(1)}, u32[]{:S(2)}, u32[]{:S(2)}) %collective-permute-start.7) | collective-permute-done | bytes 1572896 | tf_op jit(solution)/shard_map/ppermute | solution.py:30
  123.7 3.0 %collective-permute-start.9 = (bf16[384,512]{1,0:T(8,128)(2,1)S(1)}, bf16[384,512]{1,0:T(8,128)(2,1)S(1)}, u32[]{:S(2)}, u32[]{:S(2)}) collective-permute-start(bf16[384,512]{1,0:T(8,128)(2,1)S(1)} %add.374.refs_0_), channel_id=1, source_target_pairs={{0,4},{2,6},{4,0},{6,2},{1,5},{3,7},{5,1},{7,3},{8,12},{10,14},{12... | collective-permute-start | bytes 1179656 | tf_op jit(solution)/shard_map/ppermute | solution.py:34
  126.8 9.0 %corr.5 = (f32[2,128,512]{2,1,0:T(8,128)}, bf16[2,128,512]{2,1,0:T(8,128)(2,1)}) custom-call(bf16[2,128,3072]{2,1,0:T(8,128)(2,1)} %copy-done.4, bf16[2,128,3072]{2,1,0:T(8,128)(2,1)} %collective-permute-done.8.refs_1_, f32[2,3072]{1,0:T(2,128)} %pad_maximum_fusion.2.refs_2_.refs_6_, bf16[3072,1024]{1,0:T(8,128)(2,1)} %get-tuple-element.73.refs_3_.refs_7_, ...), custom_call_target="tpu_custom_call" | custom-call | flops 3221225472 | bytes 31457280 | tf_op jit(solution)/shard_map/corr/pallas_call | solution.py:174
  135.7 2.0 %collective-permute-start.13 = (bf16[2,128,512]{2,1,0:T(8,128)(2,1)}, bf16[2,128,512]{2,1,0:T(8,128)(2,1)S(1)}, u32[]{:S(2)}, u32[]{:S(2)}) collective-permute-start(bf16[2,128,512]{2,1,0:T(8,128)(2,1)} %get-tuple-element.94), channel_id=1, source_target_pairs={{0,2},{2,0},{4,6},{6,4},{1,3},{3,1},{5,7},{7,5},{8,10},{10,8},{12,... | collective-permute-start | bytes 786440 | tf_op jit(solution)/shard_map/ppermute | solution.py:34
  138.3 5.0 %collective-permute-start.11 = (bf16[256,512]{1,0:T(8,128)(2,1)S(1)}, bf16[256,512]{1,0:T(8,128)(2,1)S(1)}, u32[]{:S(2)}, u32[]{:S(2)}) collective-permute-start(bf16[256,512]{1,0:T(8,128)(2,1)S(1)} %get-tuple-element.103), channel_id=1, source_target_pairs={{0,120},{8,0},{16,8},{24,16},{32,24},{40,32},{48,40},{56,48},{64,5... | collective-permute-start | bytes 786440 | tf_op jit(solution)/shard_map/ppermute | solution.py:30
  143.7 1.3 collective-permute-start.14
  144.9 1.8 %collective-permute-start.16 = (bf16[128,512]{1,0:T(8,128)(2,1)S(1)}, bf16[128,512]{1,0:T(8,128)(2,1)S(1)}, u32[]{:S(2)}, u32[]{:S(2)}) collective-permute-start(bf16[128,512]{1,0:T(8,128)(2,1)S(1)} %get-tuple-element.96), channel_id=1, source_target_pairs={{0,5},{1,4},{2,7},{3,6},{4,1},{5,0},{6,3},{7,2},{8,13},{9,12},{10,... | collective-permute-start | bytes 393224 | tf_op jit(solution)/shard_map/ppermute | solution.py:262
  148.6 1.9 %collective-permute-start.12 = (bf16[1024,512]{1,0:T(8,128)(2,1)S(1)}, bf16[1024,512]{1,0:T(8,128)(2,1)S(1)}, u32[]{:S(2)}, u32[]{:S(2)}) collective-permute-start(bf16[1024,512]{1,0:T(8,128)(2,1)S(1)} %pad_maximum_fusion.early_ref), channel_id=1, source_target_pairs={{0,2},{2,0},{4,6},{6,4},{1,3},{3,1},{5,7},{7,5},{8,10},{10,8},{12,... | collective-permute-start | bytes 3145736 | tf_op jit(solution)/shard_map/ppermute | solution.py:34
  150.6 2.5 %collective-permute-done.15.refs_2_ = bf16[128,512]{1,0:T(8,128)(2,1)S(1)} collective-permute-done((bf16[128,512]{1,0:T(8,128)(2,1)S(1)}, bf16[128,512]{1,0:T(8,128)(2,1)S(1)}, u32[]{:S(2)}, u32[]{:S(2)}) %collective-permute-start.15) | collective-permute-done | bytes 131104 | tf_op jit(solution)/shard_map/ppermute | solution.py:34
  153.4 4.8 %collective-permute-start.18 = (bf16[128,512]{1,0:T(8,128)(2,1)S(1)}, bf16[128,512]{1,0:T(8,128)(2,1)S(1)}, u32[]{:S(2)}, u32[]{:S(2)}) collective-permute-start(bf16[128,512]{1,0:T(8,128)(2,1)S(1)} %sum.5), channel_id=1, source_target_pairs={{0,120},{8,0},{16,8},{24,16},{32,24},{40,32},{48,40},{56,48},{64,5... | collective-permute-start | bytes 393224 | tf_op jit(solution)/shard_map/ppermute | solution.py:30
  158.2 2.3 %collective-permute-done.17 = bf16[128,512]{1,0:T(8,128)(2,1)S(1)} collective-permute-done((bf16[128,512]{1,0:T(8,128)(2,1)S(1)}, bf16[128,512]{1,0:T(8,128)(2,1)S(1)}, u32[]{:S(2)}, u32[]{:S(2)}) %collective-permute-start.17) | collective-permute-done | bytes 131104 | tf_op jit(solution)/shard_map/ppermute | solution.py:30
  160.6 3.8 %collective-permute-start.19 = (bf16[256,512]{1,0:T(8,128)(2,1)S(1)}, bf16[256,512]{1,0:T(8,128)(2,1)S(1)}, u32[]{:S(2)}, u32[]{:S(2)}) collective-permute-start(bf16[256,512]{1,0:T(8,128)(2,1)S(1)} %constant_dynamic-update-slice_fusion.2.late_ref), channel_id=1, source_target_pairs={{0,2},{2,0},{4,6},{6,4},{1,3},{3,1},{5,7},{7,5},{8,10},{10,8},{12,... | collective-permute-start | bytes 786440 | tf_op jit(solution)/shard_map/ppermute | solution.py:34
  165.5 6.4 %final.1 = f32[625,2,1024]{2,1,0:T(2,128)} custom-call(s32[1]{0:T(128)} %bitcast.at_ref, s32[1,1280]{1,0:T(1,128)S(1)} %broadcast_in_dim.32.ids_ref, bf16[1024,512]{1,0:T(8,128)(2,1)S(1)} %pad_maximum_fusion.early_ref, bf16[1024,512]{1,0:T(8,128)(2,1)S(1)} %collective-permute-done.12.early2_ref, ...), custom_call_target="tpu_custom_call" | custom-call | tf_op jit(solution)/shard_map/final/pallas_call | solution.py:284
  (82 shorter events, 19.8 us)
Async XLA Ops:
  7.1 8.0 %copy-start = (bf16[1,625,2,3072]{3,1,2,0:T(8,128)(2,1)}, bf16[1,625,2,3072]{3,1,2,0:T(8,128)(2,1)S(1)}, u32[]{:S(2)}) copy-start(bf16[1,625,2,3072]{3,1,2,0:T(8,128)(2,1)S(1)} %copy.12) | copy-start | bytes 23040004
  15.1 76.4 %collective-permute-start.2 = (bf16[2,256,3072]{2,1,0:T(8,128)(2,1)}, bf16[2,256,3072]{2,1,0:T(8,128)(2,1)}, u32[]{:S(2)}, u32[]{:S(2)}) collective-permute-start(bf16[2,256,3072]{2,1,0:T(8,128)(2,1)} %get-tuple-element.79), channel_id=1, source_target_pairs={{0,8},{8,16},{16,24},{24,32},{32,40},{40,48},{48,56},{56,64},{64,7... | collective-permute-start | bytes 9437192 | tf_op jit(solution)/shard_map/ppermute | solution.py:30
  17.3 74.3 %collective-permute-start.3 = (bf16[2,256,3072]{2,1,0:T(8,128)(2,1)}, bf16[2,256,3072]{2,1,0:T(8,128)(2,1)}, u32[]{:S(2)}, u32[]{:S(2)}) collective-permute-start(bf16[2,256,3072]{2,1,0:T(8,128)(2,1)} %get-tuple-element.80), channel_id=1, source_target_pairs={{0,120},{8,0},{16,8},{24,16},{32,24},{40,32},{48,40},{56,48},{64,5... | collective-permute-start | bytes 9437192 | tf_op jit(solution)/shard_map/ppermute | solution.py:30
  28.0 9.0 %copy-start.5 = (s32[16,3]{0,1:T(4,128)S(1)}, s32[16,3]{0,1:T(4,128)}, u32[]{:S(2)}) copy-start(s32[16,3]{0,1:T(4,128)} %param.11) | copy-start | bytes 580
  68.6 16.5 %copy-start.7 = (bf16[2,128,3072]{2,1,0:T(8,128)(2,1)S(1)}, bf16[2,128,3072]{2,1,0:T(8,128)(2,1)}, u32[]{:S(2)}) copy-start(bf16[2,128,3072]{2,1,0:T(8,128)(2,1)} %get-tuple-element.88) | copy-start | bytes 4718596
  68.6 16.5 %copy-start.6 = (bf16[2,128,3072]{2,1,0:T(8,128)(2,1)S(1)}, bf16[2,128,3072]{2,1,0:T(8,128)(2,1)}, u32[]{:S(2)}) copy-start(bf16[2,128,3072]{2,1,0:T(8,128)(2,1)} %get-tuple-element.89) | copy-start | bytes 4718596
  79.7 2.7 %collective-permute-start = (bf16[2,256,512]{2,1,0:T(8,128)(2,1)}, bf16[2,256,512]{2,1,0:T(8,128)(2,1)S(1)}, u32[]{:S(2)}, u32[]{:S(2)}) collective-permute-start(bf16[2,256,512]{2,1,0:T(8,128)(2,1)} %get-tuple-element.76), channel_id=1, source_target_pairs={{0,2},{2,0},{4,6},{6,4},{1,3},{3,1},{5,7},{7,5},{8,10},{10,8},{12,... | collective-permute-start | bytes 1572872 | tf_op jit(solution)/shard_map/ppermute | solution.py:34
  82.4 1.2 copy-start.2
  83.8 7.7 %collective-permute-start.1 = (bf16[256,512]{1,0:T(8,128)(2,1)S(1)}, bf16[256,512]{1,0:T(8,128)(2,1)S(1)}, u32[]{:S(2)}, u32[]{:S(2)}) collective-permute-start(bf16[256,512]{1,0:T(8,128)(2,1)S(1)} %get-tuple-element.78), channel_id=1, source_target_pairs={{0,1},{1,0},{2,3},{3,2},{4,5},{5,4},{6,7},{7,6},{8,9},{9,8},{10,11... | collective-permute-start | bytes 786440 | tf_op jit(solution)/shard_map/ppermute | solution.py:34
  85.1 38.6 %collective-permute-start.7 = (bf16[2,128,3072]{2,1,0:T(8,128)(2,1)S(1)}, bf16[2,128,3072]{2,1,0:T(8,128)(2,1)S(1)}, u32[]{:S(2)}, u32[]{:S(2)}) collective-permute-start(bf16[2,128,3072]{2,1,0:T(8,128)(2,1)S(1)} %copy-done.7), channel_id=1, source_target_pairs={{0,8},{8,16},{16,24},{24,32},{32,40},{40,48},{48,56},{56,64},{64,7... | collective-permute-start | bytes 4718600 | tf_op jit(solution)/shard_map/ppermute | solution.py:30
  85.1 38.6 %collective-permute-start.8 = (bf16[2,128,3072]{2,1,0:T(8,128)(2,1)S(1)}, bf16[2,128,3072]{2,1,0:T(8,128)(2,1)}, u32[]{:S(2)}, u32[]{:S(2)}) collective-permute-start(bf16[2,128,3072]{2,1,0:T(8,128)(2,1)S(1)} %copy-done.6), channel_id=1, source_target_pairs={{0,120},{8,0},{16,8},{24,16},{32,24},{40,32},{48,40},{56,48},{64,5... | collective-permute-start | bytes 4718600 | tf_op jit(solution)/shard_map/ppermute | solution.py:30
  105.2 3.2 %collective-permute-start.5 = (bf16[2,384,512]{2,1,0:T(8,128)(2,1)}, bf16[2,384,512]{2,1,0:T(8,128)(2,1)S(1)}, u32[]{:S(2)}, u32[]{:S(2)}) collective-permute-start(bf16[2,384,512]{2,1,0:T(8,128)(2,1)} %get-tuple-element.85), channel_id=1, source_target_pairs={{0,2},{2,0},{4,6},{6,4},{1,3},{3,1},{5,7},{7,5},{8,10},{10,8},{12,... | collective-permute-start | bytes 2359304 | tf_op jit(solution)/shard_map/ppermute | solution.py:34
  108.4 1.4 copy-start.1
  110.0 10.5 %collective-permute-start.6 = (bf16[384,512]{1,0:T(8,128)(2,1)S(1)}, bf16[384,512]{1,0:T(8,128)(2,1)S(1)}, u32[]{:S(2)}, u32[]{:S(2)}) collective-permute-start(bf16[384,512]{1,0:T(8,128)(2,1)S(1)} %get-tuple-element.87), channel_id=1, source_target_pairs={{0,1},{1,0},{2,3},{3,2},{4,5},{5,4},{6,7},{7,6},{8,9},{9,8},{10,11... | collective-permute-start | bytes 1179656 | tf_op jit(solution)/shard_map/ppermute | solution.py:34
  123.7 3.1 %copy-start.4 = (bf16[2,128,3072]{2,1,0:T(8,128)(2,1)}, bf16[2,128,3072]{2,1,0:T(8,128)(2,1)S(1)}, u32[]{:S(2)}) copy-start(bf16[2,128,3072]{2,1,0:T(8,128)(2,1)S(1)} %collective-permute-done.7.refs_0_) | copy-start | bytes 4718596
  123.7 14.0 %collective-permute-start.9 = (bf16[384,512]{1,0:T(8,128)(2,1)S(1)}, bf16[384,512]{1,0:T(8,128)(2,1)S(1)}, u32[]{:S(2)}, u32[]{:S(2)}) collective-permute-start(bf16[384,512]{1,0:T(8,128)(2,1)S(1)} %add.374.refs_0_), channel_id=1, source_target_pairs={{0,4},{2,6},{4,0},{6,2},{1,5},{3,7},{5,1},{7,3},{8,12},{10,14},{12... | collective-permute-start | bytes 1179656 | tf_op jit(solution)/shard_map/ppermute | solution.py:34
  126.7 16.6 %collective-permute-start.4 = (bf16[256,512]{1,0:T(8,128)(2,1)S(1)}, bf16[256,512]{1,0:T(8,128)(2,1)S(1)}, u32[]{:S(2)}, u32[]{:S(2)}) collective-permute-start(bf16[256,512]{1,0:T(8,128)(2,1)S(1)} %add.373.refs_0_), channel_id=1, source_target_pairs={{0,4},{2,6},{4,0},{6,2},{1,5},{3,7},{5,1},{7,3},{8,12},{10,14},{12... | collective-permute-start | bytes 786440 | tf_op jit(solution)/shard_map/ppermute | solution.py:34
  135.7 7.9 %collective-permute-start.13 = (bf16[2,128,512]{2,1,0:T(8,128)(2,1)}, bf16[2,128,512]{2,1,0:T(8,128)(2,1)S(1)}, u32[]{:S(2)}, u32[]{:S(2)}) collective-permute-start(bf16[2,128,512]{2,1,0:T(8,128)(2,1)} %get-tuple-element.94), channel_id=1, source_target_pairs={{0,2},{2,0},{4,6},{6,4},{1,3},{3,1},{5,7},{7,5},{8,10},{10,8},{12,... | collective-permute-start | bytes 786440 | tf_op jit(solution)/shard_map/ppermute | solution.py:34
  138.1 5.5 %copy-start.3 = (f32[2,128,512]{2,1,0:T(8,128)S(1)}, f32[2,128,512]{2,1,0:T(8,128)}, u32[]{:S(2)}) copy-start(f32[2,128,512]{2,1,0:T(8,128)} %get-tuple-element.93.keep_ref) | copy-start | bytes 1572868
  138.2 10.4 %collective-permute-start.10 = (bf16[256,512]{1,0:T(8,128)(2,1)S(1)}, bf16[256,512]{1,0:T(8,128)(2,1)S(1)}, u32[]{:S(2)}, u32[]{:S(2)}) collective-permute-start(bf16[256,512]{1,0:T(8,128)(2,1)S(1)} %pad_maximum_fusion.1), channel_id=1, source_target_pairs={{0,8},{8,16},{16,24},{24,32},{32,40},{40,48},{48,56},{56,64},{64,7... | collective-permute-start | bytes 786440 | tf_op jit(solution)/shard_map/ppermute | solution.py:30
  138.3 10.3 %collective-permute-start.11 = (bf16[256,512]{1,0:T(8,128)(2,1)S(1)}, bf16[256,512]{1,0:T(8,128)(2,1)S(1)}, u32[]{:S(2)}, u32[]{:S(2)}) collective-permute-start(bf16[256,512]{1,0:T(8,128)(2,1)S(1)} %get-tuple-element.103), channel_id=1, source_target_pairs={{0,120},{8,0},{16,8},{24,16},{32,24},{40,32},{48,40},{56,48},{64,5... | collective-permute-start | bytes 786440 | tf_op jit(solution)/shard_map/ppermute | solution.py:30
  143.7 6.9 %collective-permute-start.14 = (bf16[128,512]{1,0:T(8,128)(2,1)S(1)}, bf16[128,512]{1,0:T(8,128)(2,1)S(1)}, u32[]{:S(2)}, u32[]{:S(2)}) collective-permute-start(bf16[128,512]{1,0:T(8,128)(2,1)S(1)} %get-tuple-element.96), channel_id=1, source_target_pairs={{0,1},{1,0},{2,3},{3,2},{4,5},{5,4},{6,7},{7,6},{8,9},{9,8},{10,11... | collective-permute-start | bytes 393224 | tf_op jit(solution)/shard_map/ppermute | solution.py:34
  144.9 8.1 %collective-permute-start.16 = (bf16[128,512]{1,0:T(8,128)(2,1)S(1)}, bf16[128,512]{1,0:T(8,128)(2,1)S(1)}, u32[]{:S(2)}, u32[]{:S(2)}) collective-permute-start(bf16[128,512]{1,0:T(8,128)(2,1)S(1)} %get-tuple-element.96), channel_id=1, source_target_pairs={{0,5},{1,4},{2,7},{3,6},{4,1},{5,0},{6,3},{7,2},{8,13},{9,12},{10,... | collective-permute-start | bytes 393224 | tf_op jit(solution)/shard_map/ppermute | solution.py:262
  146.8 6.3 %collective-permute-start.15 = (bf16[128,512]{1,0:T(8,128)(2,1)S(1)}, bf16[128,512]{1,0:T(8,128)(2,1)S(1)}, u32[]{:S(2)}, u32[]{:S(2)}) collective-permute-start(bf16[128,512]{1,0:T(8,128)(2,1)S(1)} %get-tuple-element.95.refs_0_), channel_id=1, source_target_pairs={{0,4},{2,6},{4,0},{6,2},{1,5},{3,7},{5,1},{7,3},{8,12},{10,14},{12... | collective-permute-start | bytes 393224 | tf_op jit(solution)/shard_map/ppermute | solution.py:34
  148.6 16.8 %collective-permute-start.12 = (bf16[1024,512]{1,0:T(8,128)(2,1)S(1)}, bf16[1024,512]{1,0:T(8,128)(2,1)S(1)}, u32[]{:S(2)}, u32[]{:S(2)}) collective-permute-start(bf16[1024,512]{1,0:T(8,128)(2,1)S(1)} %pad_maximum_fusion.early_ref), channel_id=1, source_target_pairs={{0,2},{2,0},{4,6},{6,4},{1,3},{3,1},{5,7},{7,5},{8,10},{10,8},{12,... | collective-permute-start | bytes 3145736 | tf_op jit(solution)/shard_map/ppermute | solution.py:34
  153.3 7.2 %collective-permute-start.17 = (bf16[128,512]{1,0:T(8,128)(2,1)S(1)}, bf16[128,512]{1,0:T(8,128)(2,1)S(1)}, u32[]{:S(2)}, u32[]{:S(2)}) collective-permute-start(bf16[128,512]{1,0:T(8,128)(2,1)S(1)} %sum.5), channel_id=1, source_target_pairs={{0,8},{8,16},{16,24},{24,32},{32,40},{40,48},{48,56},{56,64},{64,7... | collective-permute-start | bytes 393224 | tf_op jit(solution)/shard_map/ppermute | solution.py:30
  153.4 7.1 %collective-permute-start.18 = (bf16[128,512]{1,0:T(8,128)(2,1)S(1)}, bf16[128,512]{1,0:T(8,128)(2,1)S(1)}, u32[]{:S(2)}, u32[]{:S(2)}) collective-permute-start(bf16[128,512]{1,0:T(8,128)(2,1)S(1)} %sum.5), channel_id=1, source_target_pairs={{0,120},{8,0},{16,8},{24,16},{32,24},{40,32},{48,40},{56,48},{64,5... | collective-permute-start | bytes 393224 | tf_op jit(solution)/shard_map/ppermute | solution.py:30
  160.6 4.9 %collective-permute-start.19 = (bf16[256,512]{1,0:T(8,128)(2,1)S(1)}, bf16[256,512]{1,0:T(8,128)(2,1)S(1)}, u32[]{:S(2)}, u32[]{:S(2)}) collective-permute-start(bf16[256,512]{1,0:T(8,128)(2,1)S(1)} %constant_dynamic-update-slice_fusion.2.late_ref), channel_id=1, source_target_pairs={{0,2},{2,0},{4,6},{6,4},{1,3},{3,1},{5,7},{7,5},{8,10},{10,8},{12,... | collective-permute-start | bytes 786440 | tf_op jit(solution)/shard_map/ppermute | solution.py:34

commit v3 on v2

--- a/solution.py
+++ b/solution.py
@@ -196,14 +196,14 @@
 
 
 def fold_kernel(keep_ref, other_ref, mine_ref, far_ref):
-    mine_ref[...] = (keep_ref[0] + other_ref[0].astype(F32)).astype(BF16)
+    mine_ref[...] = (keep_ref[0] + other_ref[0].astype(F32)).astype(mine_ref.dtype)
     far_ref[...] = (keep_ref[1] + other_ref[1].astype(F32)).astype(BF16)
 
 
-def fold(keep, other):
-    shape = jax.ShapeDtypeStruct(keep.shape[1:], BF16)
-    return pl.pallas_call(
-        fold_kernel, out_shape=(shape, shape), compiler_params=params(), name="fold"
+def fold(keep, other, mine_type):
+    shapes = [jax.ShapeDtypeStruct(keep.shape[1:], kind) for kind in (mine_type, BF16)]
+    return pl.pallas_call(
+        fold_kernel, out_shape=shapes, compiler_params=params(), name="fold"
     )(keep, other)
 
 
@@ -236,9 +236,9 @@
     )(flip[None], *parts)
 
 
-def folded(partial):
+def folded(partial, mine_type=F32):
     keep, send = partial
-    return fold(keep, swapped(send, "seg", 1))
+    return fold(keep, swapped(send, "seg", 1), mine_type)
 
 
 def near_sum(mine, far):
@@ -349,7 +349,7 @@
     )
     corr1 = far_sum(both1, flip)
     tail = slots - SPLIT
-    half2 = folded(correlate([(at(above, tail, 0), at(below, tail, 0))], turn, table))
+    half2 = folded(correlate([(at(above, tail, 0), at(below, tail, 0))], turn, table), BF16)
     corr2 = direct_sum(*half2, flip)
     to_after = jnp.concatenate([corr1[:HALF], corr1[2 * HALF :]])
     to_before = corr1[HALF:]

time: 173 us -> 173 us (level)
  no operation moved by 1% of the time
where the time goes in v3:
time: 173 us; the launch traced here: 172 us
  Pallas kernels  75.6 us (44%)
  starting transfers between devices  40.8 us (24%)
  waiting for transfers between devices  22.3 us (13%)
  local copies, waits for them, and re-layouts  17.6 us (10%)
  other arithmetic  15.2 us (9%)
    pallas_call x3, Pallas kernels, correlate(): pl.pallas_call(functools.partial(corr_kernel, len(pairs)), out_shape=(jax...  33.8 us
    pallas_call x2, Pallas kernels, pick(): pl.pallas_call(pick_kernel, out_shape=[jax.ShapeDtypeStruct((2, count, fr...  22 us
    ppermute x8, starting transfers between devices, shifted(): lax.ppermute(value, 'chan', route('chan', lambda i: (i + distance) % count))  21.7 us
    ppermute x11, starting transfers between devices, swapped(): return lax.ppermute(value, axis, route(axis, lambda i: i ^ bit))  17.3 us
    ppermute x11, waiting for transfers between devices, swapped(): return lax.ppermute(value, axis, route(axis, lambda i: i ^ bit))  15.7 us
    pallas_call x1, Pallas kernels, lag_table(): pl.pallas_call(table_kernel, out_shape=[jax.ShapeDtypeStruct((freqs, 2 *...  12.1 us
    sin x2, other arithmetic, waves(): return (jnp.cos(angle), jnp.sin(angle))  9.27 us
    unnamed x29, local copies, waits for them, and re-layouts  8.9 us
  transfers between devices with their start and end apart: 20, of which 9 were waited for; matrix products, arithmetic and copies ran while one was open for 13% of the time, Pallas kernels for 36%

profile of v3, /device:TPU:1, one launch (start us, length us, event | category | flops | bytes accessed | tf_op | source)
XLA Modules:
  0.0 171.8 jit_solution(16278053576070271353)
XLA Ops:
  1.6 5.5 %copy.12 = bf16[1,625,2,3072]{3,1,2,0:T(8,128)(2,1)S(1)} copy(bf16[1,625,2,3072]{3,2,1,0:T(2,128)(2,1)} %param.6) | data formatting | bytes 15360000 | tf_op args[0]
  7.1 8.0 %pick.2 = (bf16[2,256,3072]{2,1,0:T(8,128)(2,1)}, bf16[2,256,3072]{2,1,0:T(8,128)(2,1)}) custom-call(s32[512,1]{1,0:T(8,128)S(1)} %copy.9.index_ref, bf16[2,625,3072]{2,1,0:T(8,128)(2,1)S(1)} %bitcast.43), custom_call_target="tpu_custom_call" | custom-call | flops 3932160000 | bytes 13971456 | tf_op jit(solution)/shard_map/pick/pallas_call | solution.py:70
  15.1 2.1 %collective-permute-start.2 = (bf16[2,256,3072]{2,1,0:T(8,128)(2,1)}, bf16[2,256,3072]{2,1,0:T(8,128)(2,1)}, u32[]{:S(2)}, u32[]{:S(2)}) collective-permute-start(bf16[2,256,3072]{2,1,0:T(8,128)(2,1)} %get-tuple-element.79), channel_id=1, source_target_pairs={{0,8},{8,16},{16,24},{24,32},{32,40},{40,48},{48,56},{56,64},{64,7... | collective-permute-start | bytes 9437192 | tf_op jit(solution)/shard_map/ppermute | solution.py:30
  17.3 4.9 %collective-permute-start.3 = (bf16[2,256,3072]{2,1,0:T(8,128)(2,1)}, bf16[2,256,3072]{2,1,0:T(8,128)(2,1)}, u32[]{:S(2)}, u32[]{:S(2)}) collective-permute-start(bf16[2,256,3072]{2,1,0:T(8,128)(2,1)} %get-tuple-element.80), channel_id=1, source_target_pairs={{0,120},{8,0},{16,8},{24,16},{32,24},{40,32},{48,40},{56,48},{64,5... | collective-permute-start | bytes 9437192 | tf_op jit(solution)/shard_map/ppermute | solution.py:30
  24.0 2.0 %reshape.65.cos_a_ref = f32[3072,8]{1,0:T(8,128)} reshape(f32[24576]{0:T(1024)S(1)} %get-tuple-element.54) | data formatting | bytes 196608 | tf_op jit(solution)/shard_map/reshape | solution.py:108
  26.0 2.0 %reshape.66.sin_a_ref = f32[3072,8]{1,0:T(8,128)} reshape(f32[24576]{0:T(1024)S(1)} %get-tuple-element.55) | data formatting | bytes 196608 | tf_op jit(solution)/shard_map/reshape | solution.py:108
  28.0 8.1 %fusion.4 = (f32[3072,128]{1,0:T(8,128)}, f32[3072,128]{1,0:T(8,128)}) fusion(s32[3072]{0:T(1024)S(1)} %add_add_fusion, s32[128]{0:T(128)S(1)} %multiply_add_fusion), kind=kLoop, calls=%fused_computation.7 | loop fusion | flops 3538944 | bytes 3158528 | tf_op jit(solution)/shard_map/sin | solution.py:98
  41.5 14.0 %pick.3 = (bf16[2,128,3072]{2,1,0:T(8,128)(2,1)}, bf16[2,128,3072]{2,1,0:T(8,128)(2,1)}, bf16[2,768,3072]{2,1,0:T(8,128)(2,1)}) custom-call(s32[1024,1]{1,0:T(8,128)} %copy.10.index_ref, bf16[2,625,3072]{2,1,0:T(8,128)(2,1)} %bitcast.44), custom_call_target="tpu_custom_call" | custom-call | flops 7864320000 | bytes 20262912 | tf_op jit(solution)/shard_map/pick/pallas_call | solution.py:70
  55.5 12.1 %table.1 = (bf16[3072,1024]{1,0:T(8,128)(2,1)}, bf16[3072,1024]{1,0:T(8,128)(2,1)}) custom-call(f32[3072,8]{1,0:T(8,128)} %reshape.65.cos_a_ref, f32[3072,8]{1,0:T(8,128)} %reshape.66.sin_a_ref, f32[3072,128]{1,0:T(8,128)} %get-tuple-element.71.cos_b_ref, f32[3072,128]{1,0:T(8,128)} %get-tuple-element.72.sin_b_ref, f32[1]{0:T(128)} %bitcast.27.sign_ref), custom_call_target="tpu_custom_call" | custom-call | flops 75497472 | bytes 25165824 | tf_op jit(solution)/shard_map/table/pallas_call | solution.py:116
  68.6 11.2 %corr.3 = (f32[2,256,512]{2,1,0:T(8,128)}, bf16[2,256,512]{2,1,0:T(8,128)(2,1)}) custom-call(bf16[2,768,3072]{2,1,0:T(8,128)(2,1)} %get-tuple-element.68.refs_0_.refs_1_.refs_4_, bf16[2,768,3072]{2,1,0:T(8,128)(2,1)} %get-tuple-element.68.refs_0_.refs_1_.refs_4_, f32[2,3072]{1,0:T(2,128)} %pad_maximum_fusion.2.refs_2_.refs_6_, ...), custom_call_target="tpu_custom_call" | custom-call | flops 6442450944 | bytes 37748736 | tf_op jit(solution)/shard_map/corr/pallas_call | solution.py:174
  80.7 1.7 %collective-permute-done.other_ref = bf16[2,256,512]{2,1,0:T(8,128)(2,1)S(1)} collective-permute-done((bf16[2,256,512]{2,1,0:T(8,128)(2,1)}, bf16[2,256,512]{2,1,0:T(8,128)(2,1)S(1)}, u32[]{:S(2)}, u32[]{:S(2)}) %collective-permute-start) | collective-permute-done | bytes 524320 | tf_op jit(solution)/shard_map/ppermute | solution.py:34
  83.8 1.3 collective-permute-start.1
  85.1 4.8 %collective-permute-start.8 = (bf16[2,128,3072]{2,1,0:T(8,128)(2,1)S(1)}, bf16[2,128,3072]{2,1,0:T(8,128)(2,1)}, u32[]{:S(2)}, u32[]{:S(2)}) collective-permute-start(bf16[2,128,3072]{2,1,0:T(8,128)(2,1)S(1)} %copy-done.6), channel_id=1, source_target_pairs={{0,120},{8,0},{16,8},{24,16},{32,24},{40,32},{48,40},{56,48},{64,5... | collective-permute-start | bytes 4718600 | tf_op jit(solution)/shard_map/ppermute | solution.py:30
  89.8 1.6 collective-permute-done.1.near_ref
  91.5 13.7 %corr.4 = (f32[2,384,512]{2,1,0:T(8,128)}, bf16[2,384,512]{2,1,0:T(8,128)(2,1)}) custom-call(bf16[2,768,3072]{2,1,0:T(8,128)(2,1)} %get-tuple-element.68.refs_0_.refs_1_.refs_4_, bf16[2,256,3072]{2,1,0:T(8,128)(2,1)} %collective-permute-done.2.refs_1_.refs_2_, bf16[2,256,3072]{2,1,0:T(8,128)(2,1)} %collective-permute-done.2.refs_1_.refs_2_, ...), custom_call_target="tpu_custom_call" | custom-call | flops 9663676416 | bytes 44040192 | tf_op jit(solution)/shard_map/corr/pallas_call | solution.py:174
  106.3 1.4 and_select_fusion.2
  108.4 1.4 copy-done.1
  110.0 1.3 collective-permute-start.6
  112.5 8.0 %collective-permute-done.6.near_ref = bf16[384,512]{1,0:T(8,128)(2,1)S(1)} collective-permute-done((bf16[384,512]{1,0:T(8,128)(2,1)S(1)}, bf16[384,512]{1,0:T(8,128)(2,1)S(1)}, u32[]{:S(2)}, u32[]{:S(2)}) %collective-permute-start.6) | collective-permute-done | bytes 393248 | tf_op jit(solution)/shard_map/ppermute | solution.py:34
  120.5 3.1 %collective-permute-done.7.refs_0_ = bf16[2,128,3072]{2,1,0:T(8,128)(2,1)S(1)} collective-permute-done((bf16[2,128,3072]{2,1,0:T(8,128)(2,1)S(1)}, bf16[2,128,3072]{2,1,0:T(8,128)(2,1)S(1)}, u32[]{:S(2)}, u32[]{:S(2)}) %collective-permute-start.7) | collective-permute-done | bytes 1572896 | tf_op jit(solution)/shard_map/ppermute | solution.py:30
  123.7 3.0 %collective-permute-start.9 = (bf16[384,512]{1,0:T(8,128)(2,1)S(1)}, bf16[384,512]{1,0:T(8,128)(2,1)S(1)}, u32[]{:S(2)}, u32[]{:S(2)}) collective-permute-start(bf16[384,512]{1,0:T(8,128)(2,1)S(1)} %add.374.refs_0_), channel_id=1, source_target_pairs={{0,4},{2,6},{4,0},{6,2},{1,5},{3,7},{5,1},{7,3},{8,12},{10,14},{12... | collective-permute-start | bytes 1179656 | tf_op jit(solution)/shard_map/ppermute | solution.py:34
  126.8 9.0 %corr.5 = (f32[2,128,512]{2,1,0:T(8,128)}, bf16[2,128,512]{2,1,0:T(8,128)(2,1)}) custom-call(bf16[2,128,3072]{2,1,0:T(8,128)(2,1)} %copy-done.4, bf16[2,128,3072]{2,1,0:T(8,128)(2,1)} %collective-permute-done.8.refs_1_, f32[2,3072]{1,0:T(2,128)} %pad_maximum_fusion.2.refs_2_.refs_6_, bf16[3072,1024]{1,0:T(8,128)(2,1)} %get-tuple-element.73.refs_3_.refs_7_, ...), custom_call_target="tpu_custom_call" | custom-call | flops 3221225472 | bytes 31457280 | tf_op jit(solution)/shard_map/corr/pallas_call | solution.py:174
  135.7 2.0 %collective-permute-start.13 = (bf16[2,128,512]{2,1,0:T(8,128)(2,1)}, bf16[2,128,512]{2,1,0:T(8,128)(2,1)S(1)}, u32[]{:S(2)}, u32[]{:S(2)}) collective-permute-start(bf16[2,128,512]{2,1,0:T(8,128)(2,1)} %get-tuple-element.94), channel_id=1, source_target_pairs={{0,2},{2,0},{4,6},{6,4},{1,3},{3,1},{5,7},{7,5},{8,10},{10,8},{12,... | collective-permute-start | bytes 786440 | tf_op jit(solution)/shard_map/ppermute | solution.py:34
  138.3 5.0 %collective-permute-start.11 = (bf16[256,512]{1,0:T(8,128)(2,1)S(1)}, bf16[256,512]{1,0:T(8,128)(2,1)S(1)}, u32[]{:S(2)}, u32[]{:S(2)}) collective-permute-start(bf16[256,512]{1,0:T(8,128)(2,1)S(1)} %get-tuple-element.103), channel_id=1, source_target_pairs={{0,120},{8,0},{16,8},{24,16},{32,24},{40,32},{48,40},{56,48},{64,5... | collective-permute-start | bytes 786440 | tf_op jit(solution)/shard_map/ppermute | solution.py:30
  143.7 1.3 collective-permute-start.14
  144.9 1.8 %collective-permute-start.16 = (bf16[128,512]{1,0:T(8,128)(2,1)S(1)}, bf16[128,512]{1,0:T(8,128)(2,1)S(1)}, u32[]{:S(2)}, u32[]{:S(2)}) collective-permute-start(bf16[128,512]{1,0:T(8,128)(2,1)S(1)} %get-tuple-element.96), channel_id=1, source_target_pairs={{0,5},{1,4},{2,7},{3,6},{4,1},{5,0},{6,3},{7,2},{8,13},{9,12},{10,... | collective-permute-start | bytes 393224 | tf_op jit(solution)/shard_map/ppermute | solution.py:262
  148.6 1.9 %collective-permute-start.12 = (bf16[1024,512]{1,0:T(8,128)(2,1)S(1)}, bf16[1024,512]{1,0:T(8,128)(2,1)S(1)}, u32[]{:S(2)}, u32[]{:S(2)}) collective-permute-start(bf16[1024,512]{1,0:T(8,128)(2,1)S(1)} %pad_maximum_fusion.early_ref), channel_id=1, source_target_pairs={{0,2},{2,0},{4,6},{6,4},{1,3},{3,1},{5,7},{7,5},{8,10},{10,8},{12,... | collective-permute-start | bytes 3145736 | tf_op jit(solution)/shard_map/ppermute | solution.py:34
  150.6 2.5 %collective-permute-done.15.refs_2_ = bf16[128,512]{1,0:T(8,128)(2,1)S(1)} collective-permute-done((bf16[128,512]{1,0:T(8,128)(2,1)S(1)}, bf16[128,512]{1,0:T(8,128)(2,1)S(1)}, u32[]{:S(2)}, u32[]{:S(2)}) %collective-permute-start.15) | collective-permute-done | bytes 131104 | tf_op jit(solution)/shard_map/ppermute | solution.py:34
  153.4 4.8 %collective-permute-start.18 = (bf16[128,512]{1,0:T(8,128)(2,1)S(1)}, bf16[128,512]{1,0:T(8,128)(2,1)S(1)}, u32[]{:S(2)}, u32[]{:S(2)}) collective-permute-start(bf16[128,512]{1,0:T(8,128)(2,1)S(1)} %sum.5), channel_id=1, source_target_pairs={{0,120},{8,0},{16,8},{24,16},{32,24},{40,32},{48,40},{56,48},{64,5... | collective-permute-start | bytes 393224 | tf_op jit(solution)/shard_map/ppermute | solution.py:30
  158.2 2.3 %collective-permute-done.17 = bf16[128,512]{1,0:T(8,128)(2,1)S(1)} collective-permute-done((bf16[128,512]{1,0:T(8,128)(2,1)S(1)}, bf16[128,512]{1,0:T(8,128)(2,1)S(1)}, u32[]{:S(2)}, u32[]{:S(2)}) %collective-permute-start.17) | collective-permute-done | bytes 131104 | tf_op jit(solution)/shard_map/ppermute | solution.py:30
  160.6 3.8 %collective-permute-start.19 = (bf16[256,512]{1,0:T(8,128)(2,1)S(1)}, bf16[256,512]{1,0:T(8,128)(2,1)S(1)}, u32[]{:S(2)}, u32[]{:S(2)}) collective-permute-start(bf16[256,512]{1,0:T(8,128)(2,1)S(1)} %constant_dynamic-update-slice_fusion.2.late_ref), channel_id=1, source_target_pairs={{0,2},{2,0},{4,6},{6,4},{1,3},{3,1},{5,7},{7,5},{8,10},{10,8},{12,... | collective-permute-start | bytes 786440 | tf_op jit(solution)/shard_map/ppermute | solution.py:34
  165.5 6.4 %final.1 = f32[625,2,1024]{2,1,0:T(2,128)} custom-call(s32[1]{0:T(128)} %bitcast.at_ref, s32[1,1280]{1,0:T(1,128)S(1)} %broadcast_in_dim.32.ids_ref, bf16[1024,512]{1,0:T(8,128)(2,1)S(1)} %pad_maximum_fusion.early_ref, bf16[1024,512]{1,0:T(8,128)(2,1)S(1)} %collective-permute-done.12.early2_ref, ...), custom_call_target="tpu_custom_call" | custom-call | tf_op jit(solution)/shard_map/final/pallas_call | solution.py:284
  (82 shorter events, 19.8 us)
Async XLA Ops:
  7.1 8.0 %copy-start = (bf16[1,625,2,3072]{3,1,2,0:T(8,128)(2,1)}, bf16[1,625,2,3072]{3,1,2,0:T(8,128)(2,1)S(1)}, u32[]{:S(2)}) copy-start(bf16[1,625,2,3072]{3,1,2,0:T(8,128)(2,1)S(1)} %copy.12) | copy-start | bytes 23040004
  15.1 76.4 %collective-permute-start.2 = (bf16[2,256,3072]{2,1,0:T(8,128)(2,1)}, bf16[2,256,3072]{2,1,0:T(8,128)(2,1)}, u32[]{:S(2)}, u32[]{:S(2)}) collective-permute-start(bf16[2,256,3072]{2,1,0:T(8,128)(2,1)} %get-tuple-element.79), channel_id=1, source_target_pairs={{0,8},{8,16},{16,24},{24,32},{32,40},{40,48},{48,56},{56,64},{64,7... | collective-permute-start | bytes 9437192 | tf_op jit(solution)/shard_map/ppermute | solution.py:30
  17.3 74.3 %collective-permute-start.3 = (bf16[2,256,3072]{2,1,0:T(8,128)(2,1)}, bf16[2,256,3072]{2,1,0:T(8,128)(2,1)}, u32[]{:S(2)}, u32[]{:S(2)}) collective-permute-start(bf16[2,256,3072]{2,1,0:T(8,128)(2,1)} %get-tuple-element.80), channel_id=1, source_target_pairs={{0,120},{8,0},{16,8},{24,16},{32,24},{40,32},{48,40},{56,48},{64,5... | collective-permute-start | bytes 9437192 | tf_op jit(solution)/shard_map/ppermute | solution.py:30
  28.0 9.0 %copy-start.5 = (s32[16,3]{0,1:T(4,128)S(1)}, s32[16,3]{0,1:T(4,128)}, u32[]{:S(2)}) copy-start(s32[16,3]{0,1:T(4,128)} %param.11) | copy-start | bytes 580
  68.6 16.5 %copy-start.7 = (bf16[2,128,3072]{2,1,0:T(8,128)(2,1)S(1)}, bf16[2,128,3072]{2,1,0:T(8,128)(2,1)}, u32[]{:S(2)}) copy-start(bf16[2,128,3072]{2,1,0:T(8,128)(2,1)} %get-tuple-element.88) | copy-start | bytes 4718596
  68.6 16.5 %copy-start.6 = (bf16[2,128,3072]{2,1,0:T(8,128)(2,1)S(1)}, bf16[2,128,3072]{2,1,0:T(8,128)(2,1)}, u32[]{:S(2)}) copy-start(bf16[2,128,3072]{2,1,0:T(8,128)(2,1)} %get-tuple-element.89) | copy-start | bytes 4718596
  79.7 2.7 %collective-permute-start = (bf16[2,256,512]{2,1,0:T(8,128)(2,1)}, bf16[2,256,512]{2,1,0:T(8,128)(2,1)S(1)}, u32[]{:S(2)}, u32[]{:S(2)}) collective-permute-start(bf16[2,256,512]{2,1,0:T(8,128)(2,1)} %get-tuple-element.76), channel_id=1, source_target_pairs={{0,2},{2,0},{4,6},{6,4},{1,3},{3,1},{5,7},{7,5},{8,10},{10,8},{12,... | collective-permute-start | bytes 1572872 | tf_op jit(solution)/shard_map/ppermute | solution.py:34
  82.4 1.2 copy-start.2
  83.8 7.7 %collective-permute-start.1 = (bf16[256,512]{1,0:T(8,128)(2,1)S(1)}, bf16[256,512]{1,0:T(8,128)(2,1)S(1)}, u32[]{:S(2)}, u32[]{:S(2)}) collective-permute-start(bf16[256,512]{1,0:T(8,128)(2,1)S(1)} %get-tuple-element.78), channel_id=1, source_target_pairs={{0,1},{1,0},{2,3},{3,2},{4,5},{5,4},{6,7},{7,6},{8,9},{9,8},{10,11... | collective-permute-start | bytes 786440 | tf_op jit(solution)/shard_map/ppermute | solution.py:34
  85.1 38.6 %collective-permute-start.7 = (bf16[2,128,3072]{2,1,0:T(8,128)(2,1)S(1)}, bf16[2,128,3072]{2,1,0:T(8,128)(2,1)S(1)}, u32[]{:S(2)}, u32[]{:S(2)}) collective-permute-start(bf16[2,128,3072]{2,1,0:T(8,128)(2,1)S(1)} %copy-done.7), channel_id=1, source_target_pairs={{0,8},{8,16},{16,24},{24,32},{32,40},{40,48},{48,56},{56,64},{64,7... | collective-permute-start | bytes 4718600 | tf_op jit(solution)/shard_map/ppermute | solution.py:30
  85.1 38.6 %collective-permute-start.8 = (bf16[2,128,3072]{2,1,0:T(8,128)(2,1)S(1)}, bf16[2,128,3072]{2,1,0:T(8,128)(2,1)}, u32[]{:S(2)}, u32[]{:S(2)}) collective-permute-start(bf16[2,128,3072]{2,1,0:T(8,128)(2,1)S(1)} %copy-done.6), channel_id=1, source_target_pairs={{0,120},{8,0},{16,8},{24,16},{32,24},{40,32},{48,40},{56,48},{64,5... | collective-permute-start | bytes 4718600 | tf_op jit(solution)/shard_map/ppermute | solution.py:30
  105.2 3.2 %collective-permute-start.5 = (bf16[2,384,512]{2,1,0:T(8,128)(2,1)}, bf16[2,384,512]{2,1,0:T(8,128)(2,1)S(1)}, u32[]{:S(2)}, u32[]{:S(2)}) collective-permute-start(bf16[2,384,512]{2,1,0:T(8,128)(2,1)} %get-tuple-element.85), channel_id=1, source_target_pairs={{0,2},{2,0},{4,6},{6,4},{1,3},{3,1},{5,7},{7,5},{8,10},{10,8},{12,... | collective-permute-start | bytes 2359304 | tf_op jit(solution)/shard_map/ppermute | solution.py:34
  108.4 1.4 copy-start.1
  110.0 10.5 %collective-permute-start.6 = (bf16[384,512]{1,0:T(8,128)(2,1)S(1)}, bf16[384,512]{1,0:T(8,128)(2,1)S(1)}, u32[]{:S(2)}, u32[]{:S(2)}) collective-permute-start(bf16[384,512]{1,0:T(8,128)(2,1)S(1)} %get-tuple-element.87), channel_id=1, source_target_pairs={{0,1},{1,0},{2,3},{3,2},{4,5},{5,4},{6,7},{7,6},{8,9},{9,8},{10,11... | collective-permute-start | bytes 1179656 | tf_op jit(solution)/shard_map/ppermute | solution.py:34
  123.7 3.1 %copy-start.4 = (bf16[2,128,3072]{2,1,0:T(8,128)(2,1)}, bf16[2,128,3072]{2,1,0:T(8,128)(2,1)S(1)}, u32[]{:S(2)}) copy-start(bf16[2,128,3072]{2,1,0:T(8,128)(2,1)S(1)} %collective-permute-done.7.refs_0_) | copy-start | bytes 4718596
  123.7 14.0 %collective-permute-start.9 = (bf16[384,512]{1,0:T(8,128)(2,1)S(1)}, bf16[384,512]{1,0:T(8,128)(2,1)S(1)}, u32[]{:S(2)}, u32[]{:S(2)}) collective-permute-start(bf16[384,512]{1,0:T(8,128)(2,1)S(1)} %add.374.refs_0_), channel_id=1, source_target_pairs={{0,4},{2,6},{4,0},{6,2},{1,5},{3,7},{5,1},{7,3},{8,12},{10,14},{12... | collective-permute-start | bytes 1179656 | tf_op jit(solution)/shard_map/ppermute | solution.py:34
  126.7 16.6 %collective-permute-start.4 = (bf16[256,512]{1,0:T(8,128)(2,1)S(1)}, bf16[256,512]{1,0:T(8,128)(2,1)S(1)}, u32[]{:S(2)}, u32[]{:S(2)}) collective-permute-start(bf16[256,512]{1,0:T(8,128)(2,1)S(1)} %add.373.refs_0_), channel_id=1, source_target_pairs={{0,4},{2,6},{4,0},{6,2},{1,5},{3,7},{5,1},{7,3},{8,12},{10,14},{12... | collective-permute-start | bytes 786440 | tf_op jit(solution)/shard_map/ppermute | solution.py:34
  135.7 7.9 %collective-permute-start.13 = (bf16[2,128,512]{2,1,0:T(8,128)(2,1)}, bf16[2,128,512]{2,1,0:T(8,128)(2,1)S(1)}, u32[]{:S(2)}, u32[]{:S(2)}) collective-permute-start(bf16[2,128,512]{2,1,0:T(8,128)(2,1)} %get-tuple-element.94), channel_id=1, source_target_pairs={{0,2},{2,0},{4,6},{6,4},{1,3},{3,1},{5,7},{7,5},{8,10},{10,8},{12,... | collective-permute-start | bytes 786440 | tf_op jit(solution)/shard_map/ppermute | solution.py:34
  138.1 5.5 %copy-start.3 = (f32[2,128,512]{2,1,0:T(8,128)S(1)}, f32[2,128,512]{2,1,0:T(8,128)}, u32[]{:S(2)}) copy-start(f32[2,128,512]{2,1,0:T(8,128)} %get-tuple-element.93.keep_ref) | copy-start | bytes 1572868
  138.2 10.4 %collective-permute-start.10 = (bf16[256,512]{1,0:T(8,128)(2,1)S(1)}, bf16[256,512]{1,0:T(8,128)(2,1)S(1)}, u32[]{:S(2)}, u32[]{:S(2)}) collective-permute-start(bf16[256,512]{1,0:T(8,128)(2,1)S(1)} %pad_maximum_fusion.1), channel_id=1, source_target_pairs={{0,8},{8,16},{16,24},{24,32},{32,40},{40,48},{48,56},{56,64},{64,7... | collective-permute-start | bytes 786440 | tf_op jit(solution)/shard_map/ppermute | solution.py:30
  138.3 10.3 %collective-permute-start.11 = (bf16[256,512]{1,0:T(8,128)(2,1)S(1)}, bf16[256,512]{1,0:T(8,128)(2,1)S(1)}, u32[]{:S(2)}, u32[]{:S(2)}) collective-permute-start(bf16[256,512]{1,0:T(8,128)(2,1)S(1)} %get-tuple-element.103), channel_id=1, source_target_pairs={{0,120},{8,0},{16,8},{24,16},{32,24},{40,32},{48,40},{56,48},{64,5... | collective-permute-start | bytes 786440 | tf_op jit(solution)/shard_map/ppermute | solution.py:30
  143.7 6.9 %collective-permute-start.14 = (bf16[128,512]{1,0:T(8,128)(2,1)S(1)}, bf16[128,512]{1,0:T(8,128)(2,1)S(1)}, u32[]{:S(2)}, u32[]{:S(2)}) collective-permute-start(bf16[128,512]{1,0:T(8,128)(2,1)S(1)} %get-tuple-element.96), channel_id=1, source_target_pairs={{0,1},{1,0},{2,3},{3,2},{4,5},{5,4},{6,7},{7,6},{8,9},{9,8},{10,11... | collective-permute-start | bytes 393224 | tf_op jit(solution)/shard_map/ppermute | solution.py:34
  144.9 8.1 %collective-permute-start.16 = (bf16[128,512]{1,0:T(8,128)(2,1)S(1)}, bf16[128,512]{1,0:T(8,128)(2,1)S(1)}, u32[]{:S(2)}, u32[]{:S(2)}) collective-permute-start(bf16[128,512]{1,0:T(8,128)(2,1)S(1)} %get-tuple-element.96), channel_id=1, source_target_pairs={{0,5},{1,4},{2,7},{3,6},{4,1},{5,0},{6,3},{7,2},{8,13},{9,12},{10,... | collective-permute-start | bytes 393224 | tf_op jit(solution)/shard_map/ppermute | solution.py:262
  146.8 6.3 %collective-permute-start.15 = (bf16[128,512]{1,0:T(8,128)(2,1)S(1)}, bf16[128,512]{1,0:T(8,128)(2,1)S(1)}, u32[]{:S(2)}, u32[]{:S(2)}) collective-permute-start(bf16[128,512]{1,0:T(8,128)(2,1)S(1)} %get-tuple-element.95.refs_0_), channel_id=1, source_target_pairs={{0,4},{2,6},{4,0},{6,2},{1,5},{3,7},{5,1},{7,3},{8,12},{10,14},{12... | collective-permute-start | bytes 393224 | tf_op jit(solution)/shard_map/ppermute | solution.py:34
  148.6 16.8 %collective-permute-start.12 = (bf16[1024,512]{1,0:T(8,128)(2,1)S(1)}, bf16[1024,512]{1,0:T(8,128)(2,1)S(1)}, u32[]{:S(2)}, u32[]{:S(2)}) collective-permute-start(bf16[1024,512]{1,0:T(8,128)(2,1)S(1)} %pad_maximum_fusion.early_ref), channel_id=1, source_target_pairs={{0,2},{2,0},{4,6},{6,4},{1,3},{3,1},{5,7},{7,5},{8,10},{10,8},{12,... | collective-permute-start | bytes 3145736 | tf_op jit(solution)/shard_map/ppermute | solution.py:34
  153.3 7.2 %collective-permute-start.17 = (bf16[128,512]{1,0:T(8,128)(2,1)S(1)}, bf16[128,512]{1,0:T(8,128)(2,1)S(1)}, u32[]{:S(2)}, u32[]{:S(2)}) collective-permute-start(bf16[128,512]{1,0:T(8,128)(2,1)S(1)} %sum.5), channel_id=1, source_target_pairs={{0,8},{8,16},{16,24},{24,32},{32,40},{40,48},{48,56},{56,64},{64,7... | collective-permute-start | bytes 393224 | tf_op jit(solution)/shard_map/ppermute | solution.py:30
  153.4 7.1 %collective-permute-start.18 = (bf16[128,512]{1,0:T(8,128)(2,1)S(1)}, bf16[128,512]{1,0:T(8,128)(2,1)S(1)}, u32[]{:S(2)}, u32[]{:S(2)}) collective-permute-start(bf16[128,512]{1,0:T(8,128)(2,1)S(1)} %sum.5), channel_id=1, source_target_pairs={{0,120},{8,0},{16,8},{24,16},{32,24},{40,32},{48,40},{56,48},{64,5... | collective-permute-start | bytes 393224 | tf_op jit(solution)/shard_map/ppermute | solution.py:30
  160.6 4.9 %collective-permute-start.19 = (bf16[256,512]{1,0:T(8,128)(2,1)S(1)}, bf16[256,512]{1,0:T(8,128)(2,1)S(1)}, u32[]{:S(2)}, u32[]{:S(2)}) collective-permute-start(bf16[256,512]{1,0:T(8,128)(2,1)S(1)} %constant_dynamic-update-slice_fusion.2.late_ref), channel_id=1, source_target_pairs={{0,2},{2,0},{4,6},{6,4},{1,3},{3,1},{5,7},{7,5},{8,10},{10,8},{12,... | collective-permute-start | bytes 786440 | tf_op jit(solution)/shard_map/ppermute | solution.py:34
